TPU v7x, 32 devices: a whole 2x2x4 slice. The times are simulated.
32 devices in a mesh: shard: 2 (over x), ctx: 4 (over z), tp: 4 (over y, core).
Axes of the slice: x: 2, y: 2, z: 4, core: 2. Of those that a mesh axis runs over, the one named last changes fastest.
Arguments:
- tokens: bfloat16 [8, 2048, 768], P('shard', 'ctx'), may hold values from -6 to 6
- segments: int32 [8, 2048], P('shard', 'ctx'), may hold values from 0 to 3, as said below
- timesteps: int32 [8], P('shard'), may hold values from 0 to 1999
- w_time1: bfloat16 [128, 768], P('shard'), may hold values from -0.75 to 0.75
- w_time2: bfloat16 [768, 768], P('shard'), may hold values from -0.21875 to 0.21875
- w_qkv: bfloat16 [768, 3, 768], P('shard', None, 'tp'), may hold values from -0.21875 to 0.21875
- w_out: bfloat16 [768, 768], P(('tp', 'shard')), may hold values from -2.5 to 2.5
- w_in: bfloat16 [768, 3072], P('shard', 'tp'), may hold values from -0.21875 to 0.21875
- w_down: bfloat16 [3072, 768], P(('tp', 'shard')), may hold values from -0.15625 to 0.15625
- norm_gains: bfloat16 [768, 2], P('shard'), may hold values from 0.3984375 to 1.59375
- norm_shifts: bfloat16 [768, 2], P('shard'), may hold values from -1.5 to 1.5
- cotangent: bfloat16 [8, 2048, 768], P('shard', 'ctx'), may hold values from -6 to 6
Outputs:
- output: bfloat16 [8, 2048, 768], P('shard', 'ctx')
- grad_tokens: float32 [8, 2048, 768], P('shard', 'ctx')
- grad_time1: float32 [128, 768], P('shard')
- grad_time2: float32 [768, 768], P('shard')
- grad_qkv: float32 [768, 3, 768], P('shard', None, 'tp')
- grad_out: float32 [768, 768], P(('tp', 'shard'))
- grad_in: float32 [768, 3072], P('shard', 'tp')
- grad_down: float32 [3072, 768], P(('tp', 'shard'))
- grad_gains: float32 [768, 2], P('shard')
- grad_shifts: float32 [768, 2], P('shard')
Inputs may be any that keep to these rules, and one draw needn't show every extreme that they name: `segments`: along each sequence the numbers never fall; a sequence holds two to four documents, each one run of 200 or more positions.
All inputs are finite; a program needn't handle non-finite values.
Results may differ from a plain program's by a relative error of at most 0.022.
Values may be sent and summed in bfloat16 or wider, within the bound.
A program may use at most 192 MiB of HBM per device.

v0:
```python
import math

import jax
import jax.numpy as jnp
from jax import lax
from jax.sharding import PartitionSpec as P

HEAD_DIM = 64


NORM_EPS = 1e-05
MASKED = -1000000000.0


def time_features(steps_in, width):
    half = width // 2
    ratios = jnp.exp(-math.log(10000.0) * jnp.arange(half, dtype=jnp.float32) / half)
    angles = steps_in.astype(jnp.float32)[:, None] * ratios[None, :]
    return jnp.concatenate([jnp.cos(angles), jnp.sin(angles)], axis=1)


def silu_fn(value):
    return value / (1.0 + jnp.exp(-value))


def gelu_fn(value):
    return 0.5 * value * (1.0 + lax.erf(value * (1.0 / math.sqrt(2.0))))


def norm_forward(rows, gain, shift):
    mean = jnp.mean(rows, axis=-1, keepdims=True)
    centred = rows - mean
    inverse = lax.rsqrt(jnp.mean(centred * centred, axis=-1, keepdims=True) + NORM_EPS)
    normed = centred * inverse
    return (normed * gain + shift, normed, inverse)


def norm_backward(grad, normed, inverse, gain):
    scaled = grad * gain
    grad_rows = inverse * (
        scaled
        - jnp.mean(scaled, axis=-1, keepdims=True)
        - normed * jnp.mean(scaled * normed, axis=-1, keepdims=True)
    )
    return (grad_rows, jnp.sum(grad * normed, axis=0), jnp.sum(grad, axis=0))


def inner_rows(left, right):
    return lax.dot_general(
        left, right, (((0,), (0,)), ((), ())), preferred_element_type=jnp.float32
    )


def times_transpose(left, right):
    return lax.dot_general(
        left, right, (((1,), (1,)), ((), ())), preferred_element_type=jnp.float32
    )


def body(
    tokens,
    segments,
    timesteps,
    w_time1,
    w_time2,
    w_qkv,
    w_out,
    w_in,
    w_down,
    norm_gains,
    norm_shifts,
    cotangent,
):
    seq_count, local_len, width = tokens.shape
    batches = seq_count // 2
    rows = 2 * local_len
    shard_size = lax.axis_size("shard")
    lead_share = (lax.axis_index("ctx") == 0).astype(jnp.float32)
    head_size = HEAD_DIM
    local_width = w_qkv.shape[2]
    local_heads = local_width // head_size
    scale = head_size ** (-0.5)
    local_weights = (w_time1, w_time2, w_qkv, w_out, w_in, w_down, norm_gains, norm_shifts)

    def summed(terms_fn):
        return lax.psum(terms_fn(0, rows).astype(jnp.bfloat16), "tp").astype(jnp.float32)

    def step(carry, slab):
        seq_tokens, seq_docs, seq_steps, seq_cot = slab
        gathered = (
            lax.all_gather(local_weights[0], "shard", axis=0, tiled=True),
            lax.all_gather(local_weights[1], "shard", axis=0, tiled=True),
            lax.all_gather(local_weights[2], "shard", axis=0, tiled=True),
            lax.all_gather(local_weights[3], "shard", axis=0, tiled=True),
            lax.all_gather(local_weights[4], "shard", axis=0, tiled=True),
            lax.all_gather(local_weights[5], "shard", axis=0, tiled=True),
            lax.all_gather(local_weights[6], "shard", axis=0, tiled=True),
            lax.all_gather(local_weights[7], "shard", axis=0, tiled=True),
        )
        time_one, time_two, joint_w, out_w, in_w, down_w, gains_low, shifts_low = gathered
        gains = gains_low.astype(jnp.float32)
        shifts = shifts_low.astype(jnp.float32)
        joint_flat = joint_w.reshape(width, 3 * local_width)
        feats = time_features(seq_steps, time_one.shape[0]).astype(jnp.bfloat16)
        time_pre = jnp.dot(feats, time_one, preferred_element_type=jnp.float32)
        time_hidden = silu_fn(time_pre).astype(jnp.bfloat16)
        time_embed = jnp.dot(time_hidden, time_two, preferred_element_type=jnp.float32)
        mixed = (seq_tokens.astype(jnp.float32) + time_embed[:, None, :]).reshape(rows, width)
        mixed_low = mixed.astype(jnp.bfloat16)
        joint = jnp.dot(mixed_low, joint_flat, preferred_element_type=jnp.float32).astype(
            jnp.bfloat16
        )
        queries = joint[:, :local_width].reshape(2, local_len, local_heads, head_size)
        own_keys = joint[:, local_width : 2 * local_width].reshape(2, local_len, local_width)
        own_values = joint[:, 2 * local_width :].reshape(2, local_len, local_width)
        keys_all, values_all, docs_all = (
            lax.all_gather(own_keys, "ctx", axis=1, tiled=True),
            lax.all_gather(own_values, "ctx", axis=1, tiled=True),
            lax.all_gather(seq_docs.astype(jnp.bfloat16), "ctx", axis=1, tiled=True),
        )
        full_len = keys_all.shape[1]
        keys_all = keys_all.reshape(2, full_len, local_heads, head_size)
        values_all = values_all.reshape(2, full_len, local_heads, head_size)
        same = (
            seq_docs.astype(jnp.float32)[:, None, :, None]
            == docs_all.astype(jnp.float32)[:, None, None, :]
        )

        def masked_scores():
            raw = (
                jnp.einsum("sqhd,skhd->shqk", queries, keys_all, preferred_element_type=jnp.float32)
                * scale
            )
            return jnp.where(same, raw, MASKED)

        scores = masked_scores()
        top = jnp.max(scores, axis=-1, keepdims=True)
        expd = jnp.exp(scores - top)
        total = jnp.sum(expd, axis=-1, keepdims=True)
        probs = expd / total
        log_total = top + jnp.log(total)
        attended = (
            jnp.einsum(
                "shqk,skhd->sqhd",
                probs.astype(jnp.bfloat16),
                values_all,
                preferred_element_type=jnp.float32,
            )
            .astype(jnp.bfloat16)
            .reshape(rows, local_width)
        )

        def attention_terms(start, count):
            return jnp.dot(attended, out_w, preferred_element_type=jnp.float32)

        branch = summed(attention_terms)
        first, first_normed, first_inverse = norm_forward(mixed + branch, gains[:, 0], shifts[:, 0])
        first_low = first.astype(jnp.bfloat16)
        inner = jnp.dot(first_low, in_w, preferred_element_type=jnp.float32)
        activated = gelu_fn(inner).astype(jnp.bfloat16)

        def feed_terms(start, count):
            return jnp.dot(activated, down_w, preferred_element_type=jnp.float32)

        second = first + summed(feed_terms)
        output, second_normed, second_inverse = norm_forward(second, gains[:, 1], shifts[:, 1])
        result = output.astype(jnp.bfloat16).reshape(2, local_len, width)
        grad_rows = seq_cot.reshape(rows, width).astype(jnp.float32)
        grad_second, grad_gain_two, grad_shift_two = norm_backward(
            grad_rows, second_normed, second_inverse, gains[:, 1]
        )
        second_low = grad_second.astype(jnp.bfloat16)
        grad_activated = times_transpose(second_low, down_w)
        gelu_pull = jax.vjp(gelu_fn, inner)[1]
        grad_inner = gelu_pull(grad_activated)[0].astype(jnp.bfloat16)
        grad_down_w = inner_rows(activated, second_low)
        grad_in_w = inner_rows(first_low, grad_inner)

        def feed_back_terms(start, count):
            return times_transpose(grad_inner, in_w)

        grad_first = grad_second + summed(feed_back_terms)
        grad_joint_sum, grad_gain_one, grad_shift_one = norm_backward(
            grad_first, first_normed, first_inverse, gains[:, 0]
        )
        branch_low = grad_joint_sum.astype(jnp.bfloat16)
        grad_out_w = inner_rows(attended, branch_low)
        grad_attended = (
            times_transpose(branch_low, out_w)
            .astype(jnp.bfloat16)
            .reshape(2, local_len, local_heads, head_size)
        )
        probs_again = jnp.exp(masked_scores() - log_total)
        grad_probs = jnp.einsum(
            "sqhd,skhd->shqk", grad_attended, values_all, preferred_element_type=jnp.float32
        )
        centre = jnp.sum(probs_again * grad_probs, axis=-1, keepdims=True)
        grad_scores = (probs_again * (grad_probs - centre)).astype(jnp.bfloat16)
        grad_queries = (
            jnp.einsum("shqk,skhd->sqhd", grad_scores, keys_all, preferred_element_type=jnp.float32)
            * scale
        ).astype(jnp.bfloat16)
        key_terms = (
            jnp.einsum("shqk,sqhd->skhd", grad_scores, queries, preferred_element_type=jnp.float32)
            * scale
        )
        value_terms = jnp.einsum(
            "shqk,sqhd->skhd",
            probs_again.astype(jnp.bfloat16),
            grad_attended,
            preferred_element_type=jnp.float32,
        )
        grad_keys, grad_values = (
            lax.psum_scatter(
                key_terms.astype(jnp.bfloat16), "ctx", scatter_dimension=1, tiled=True
            ).astype(jnp.float32),
            lax.psum_scatter(
                value_terms.astype(jnp.bfloat16), "ctx", scatter_dimension=1, tiled=True
            ).astype(jnp.float32),
        )
        grad_joint = jnp.concatenate(
            [
                grad_queries.reshape(rows, local_width),
                grad_keys.astype(jnp.bfloat16).reshape(rows, local_width),
                grad_values.astype(jnp.bfloat16).reshape(rows, local_width),
            ],
            axis=1,
        )
        grad_joint_w = inner_rows(mixed_low, grad_joint).reshape(width, 3, local_width)

        def input_terms(start, count):
            return times_transpose(grad_joint, joint_flat)

        grad_mixed = grad_joint_sum + summed(input_terms)
        grad_tokens = grad_mixed.reshape(2, local_len, width)
        grad_embed = lax.psum(jnp.sum(grad_tokens, axis=1), "ctx").astype(jnp.bfloat16)
        grad_time_two = inner_rows(time_hidden, grad_embed) * lead_share
        silu_pull = jax.vjp(silu_fn, time_pre)[1]
        grad_pre = silu_pull(times_transpose(grad_embed, time_two))[0].astype(jnp.bfloat16)
        grad_time_one = inner_rows(feats, grad_pre) * lead_share
        grad_gain_pair = jnp.stack([grad_gain_one, grad_gain_two], axis=1)
        grad_shift_pair = jnp.stack([grad_shift_one, grad_shift_two], axis=1)
        fresh = (
            grad_time_one,
            grad_time_two,
            grad_joint_w,
            grad_out_w,
            grad_in_w,
            grad_down_w,
            grad_gain_pair,
            grad_shift_pair,
        )
        carry = tuple((held + new for held, new in zip(carry, fresh)))
        return (carry, (result, grad_tokens))

    start_grads = (
        jnp.zeros((w_time1.shape[0] * shard_size, width), jnp.float32),
        jnp.zeros((w_time2.shape[0] * shard_size, width), jnp.float32),
        jnp.zeros((w_qkv.shape[0] * shard_size, 3, local_width), jnp.float32),
        jnp.zeros((w_out.shape[0] * shard_size, width), jnp.float32),
        jnp.zeros((w_in.shape[0] * shard_size, w_in.shape[1]), jnp.float32),
        jnp.zeros((w_down.shape[0] * shard_size, width), jnp.float32),
        jnp.zeros((norm_gains.shape[0] * shard_size, 2), jnp.float32),
        jnp.zeros((norm_shifts.shape[0] * shard_size, 2), jnp.float32),
    )
    slabs = (
        tokens.reshape(batches, 2, local_len, width),
        segments.reshape(batches, 2, local_len),
        timesteps.reshape(batches, 2),
        cotangent.reshape(batches, 2, local_len, width),
    )
    summed_grads, stacked = lax.scan(step, start_grads, slabs)
    results, grad_stack = stacked
    result = results.reshape(seq_count, local_len, width)
    grad_tokens = grad_stack.reshape(seq_count, local_len, width)
    gain_total, shift_total = (summed_grads[6], summed_grads[7])
    local_grads = (
        summed_grads[0],
        summed_grads[1],
        summed_grads[2],
        summed_grads[3],
        summed_grads[4],
        summed_grads[5],
        gain_total,
        shift_total,
    )
    pieces = (
        lax.psum_scatter(
            local_grads[0].astype(jnp.bfloat16), "shard", scatter_dimension=0, tiled=True
        ).astype(jnp.float32),
        lax.psum_scatter(
            local_grads[1].astype(jnp.bfloat16), "shard", scatter_dimension=0, tiled=True
        ).astype(jnp.float32),
        lax.psum_scatter(
            local_grads[2].astype(jnp.bfloat16), "shard", scatter_dimension=0, tiled=True
        ).astype(jnp.float32),
        lax.psum_scatter(
            local_grads[3].astype(jnp.bfloat16), "shard", scatter_dimension=0, tiled=True
        ).astype(jnp.float32),
        lax.psum_scatter(
            local_grads[4].astype(jnp.bfloat16), "shard", scatter_dimension=0, tiled=True
        ).astype(jnp.float32),
        lax.psum_scatter(
            local_grads[5].astype(jnp.bfloat16), "shard", scatter_dimension=0, tiled=True
        ).astype(jnp.float32),
        lax.psum_scatter(
            local_grads[6].astype(jnp.bfloat16), "shard", scatter_dimension=0, tiled=True
        ).astype(jnp.float32),
        lax.psum_scatter(
            local_grads[7].astype(jnp.bfloat16), "shard", scatter_dimension=0, tiled=True
        ).astype(jnp.float32),
    )
    pieces = (
        lax.psum(pieces[0].astype(jnp.bfloat16), "ctx").astype(jnp.float32),
        lax.psum(pieces[1].astype(jnp.bfloat16), "ctx").astype(jnp.float32),
        lax.psum(pieces[2].astype(jnp.bfloat16), "ctx").astype(jnp.float32),
        lax.psum(pieces[3].astype(jnp.bfloat16), "ctx").astype(jnp.float32),
        lax.psum(pieces[4].astype(jnp.bfloat16), "ctx").astype(jnp.float32),
        lax.psum(pieces[5].astype(jnp.bfloat16), "ctx").astype(jnp.float32),
        lax.psum(pieces[6].astype(jnp.bfloat16), "ctx").astype(jnp.float32),
        lax.psum(pieces[7].astype(jnp.bfloat16), "ctx").astype(jnp.float32),
    )
    return (
        result,
        grad_tokens,
        pieces[0],
        pieces[1],
        pieces[2],
        pieces[3],
        pieces[4],
        pieces[5],
        pieces[6],
        pieces[7],
    )


def solution(mesh):
    placed = (
        P("shard", "ctx", None),
        P("shard", "ctx"),
        P("shard"),
        P("shard", None),
        P("shard", None),
        P("shard", None, "tp"),
        P(("tp", "shard"), None),
        P("shard", "tp"),
        P(("tp", "shard"), None),
        P("shard", None),
        P("shard", None),
        P("shard", "ctx", None),
    )
    return jax.shard_map(
        body,
        mesh=mesh,
        in_specs=placed,
        out_specs=(
            P("shard", "ctx", None),
            P("shard", "ctx", None),
            P("shard", None),
            P("shard", None),
            P("shard", None, "tp"),
            P(("tp", "shard"), None),
            P("shard", "tp"),
            P(("tp", "shard"), None),
            P("shard", None),
            P("shard", None),
        ),
        check_vma=False,
    )
```

profile of v0, /device:TPU:0, one launch (start us, length us, event | category | flops | bytes accessed | tf_op | source)
XLA Modules:
  0.0 1272.0 jit_solution(966449086092957624)
XLA Ops:
  10.7 992.0 %while.31 = (s32[]{:T(128)}, f32[128,768]{1,0:T(8,128)}, f32[768,768]{1,0:T(8,128)}, f32[768,3,192]{0,2,1:T(8,128)}, f32[192,768]{1,0:T(8,128)}, /*index=5*/f32[...) while((s32[]{:T(128)}, f32[128,768]{1,0:T(8,128)}, ...), condition=%wide.region_24.25_spmd.clone, body=%wide.region_0.24_spmd.clone.sunk | while | flops 15913922560 | bytes 860398208 | solution.py:272
  11.5 6.8 all_gather.86
  19.0 22.2 %all_gather.88 = bf16[768,3,192]{0,2,1:T(8,128)(2,1)} all-gather(bf16[384,3,192]{0,2,1:T(8,128)(2,1)} %get-tuple-element.776), channel_id=1, replica_groups=mesh['shard'=2,'ctx'=4,'tp'=4] {'shard'}, dimensions={0}, use_global_device_ids=true | all-gather | bytes 1327104 | tf_op jit(solution)/shard_map/while/body/eval_jaxpr/all_gather | solution.py:93
  50.3 12.3 all-gather.3
  62.6 5.9 all_gather.91
  71.3 16.5 %all-gather.14.cloned.1.call-done = bf16[2,2048,192]{1,0,2:T(2,128)(2,1)} async-done(((bf16[2,512,192]{1,0,2:T(2,128)(2,1)}), bf16[2,2048,192]{1,0,2:T(2,128)(2,1)}) %all-gather.14.cloned.1.call-update) | async-done | bytes 1572880 | tf_op jit(solution)/shard_map/while/body/eval_jaxpr/all_gather | solution.py:117
  89.8 11.1 fusion.198
  100.9 10.5 fusion.199
  111.4 14.4 %all-gather.12.cloned.1.call-done = bf16[2,2048,192]{1,0,2:T(2,128)(2,1)} async-done(((bf16[2,512,192]{1,0,2:T(2,128)(2,1)}), bf16[2,2048,192]{1,0,2:T(2,128)(2,1)}) %all-gather.12.cloned.1.call-update) | async-done | bytes 1572880 | tf_op jit(solution)/shard_map/while/body/eval_jaxpr/all_gather | solution.py:118
  127.9 11.1 fusion.200
  145.2 4.3 all_gather.93
  150.2 4.3 all_gather.94
  154.6 28.8 %all-reduce.10.cloned.1.call-done = bf16[1024,768]{1,0:T(8,128)(2,1)} async-done(((bf16[1024,768]{1,0:T(8,128)(2,1)}), bf16[1024,768]{1,0:T(8,128)(2,1)}) %all-reduce.10.cloned.1.call-update) | async-done | bytes 1572880 | tf_op jit(solution)/shard_map/while/body/eval_jaxpr/psum | solution.py:86
  186.8 20.8 %all-gather.16.cloned.1.call-done = bf16[768,768]{1,0:T(8,128)(2,1)} async-done(((bf16[384,768]{1,0:T(8,128)(2,1)}), bf16[768,768]{1,0:T(8,128)(2,1)}) %all-gather.16.cloned.1.call-update) | async-done | bytes 1179664 | tf_op jit(solution)/shard_map/while/body/eval_jaxpr/all_gather | solution.py:95
  207.6 5.1 multiply_convert_fusion.5
  212.7 19.1 %all-gather.18.cloned.1.call-done = bf16[768,768]{1,0:T(8,128)(2,1)} async-done(((bf16[384,768]{1,0:T(8,128)(2,1)}), bf16[768,768]{1,0:T(8,128)(2,1)}) %all-gather.18.cloned.1.call-update) | async-done | bytes 1179664 | tf_op jit(solution)/shard_map/while/body/eval_jaxpr/all_gather | solution.py:96
  231.8 4.3 convolution_convert_fusion.14
  239.9 39.3 %all-reduce.12.cloned.1.call-done = bf16[1024,768]{1,0:T(8,128)(2,1)} async-done(((bf16[1024,768]{1,0:T(8,128)(2,1)}), bf16[1024,768]{1,0:T(8,128)(2,1)}) %all-reduce.12.cloned.1.call-update) | async-done | bytes 1572880 | tf_op jit(solution)/shard_map/while/body/eval_jaxpr/psum | solution.py:86
  295.0 42.3 %all-reduce.14.cloned.1.call-done = bf16[1024,768]{1,0:T(8,128)(2,1)} async-done(((bf16[1024,768]{1,0:T(8,128)(2,1)}), bf16[1024,768]{1,0:T(8,128)(2,1)}) %all-reduce.14.cloned.1.call-update) | async-done | bytes 1572880 | tf_op jit(solution)/shard_map/while/body/eval_jaxpr/psum | solution.py:86
  345.2 11.7 fusion.206
  357.0 19.7 %multiply_reduce_fusion.13 = (f32[2,3,512]{2,1,0:T(4,128)S(1)}, f32[2,3,512,2048]{3,2,1,0:T(8,128)}) fusion(f32[2,3,512,2048]{3,2,1,0:T(8,128)} %get-tuple-element.679, f32[2,3,512]{2,1,0:T(4,128)S(1)} %log_add_fusion.2, bf16[2,2048,3,64]{1,3,2,0:T(8,128)(2,1)S(1)} %bitcast.245, bf16[2,512,3,64]{1,0,3,2:T(2,128)(2,1)S(1)} %reshape.329), kind=kOutput, calls=%fused_computation.1.clone.1 | convolution fusion | flops 824177664 | bytes 52322304 | tf_op jit(solution)/shard_map/while/body/eval_jaxpr/sqhd,skhd->shqk/dot_general | solution.py:194
  376.8 16.8 %multiply_convert_fusion.6 = bf16[2,3,512,2048]{3,2,1,0:T(8,128)(2,1)S(1)} fusion(f32[2,3,512,2048]{3,2,1,0:T(8,128)} %get-tuple-element.698, f32[2,3,512,2048]{3,2,1,0:T(8,128)} %get-tuple-element.679, f32[2,3,512]{2,1,0:T(4,128)S(1)} %get-tuple-element.699, f32[2,3,512]{2,1,0:T(4,128)S(1)} %log_add_fusion.2), kind=kLoop, calls=%fused_computation.clone.1 | loop fusion | flops 25165824 | bytes 62939136 | tf_op jit(solution)/shard_map/while/body/eval_jaxpr/convert_element_type | solution.py:198
  393.6 4.5 copy-done
  407.7 4.8 select_add_fusion.10
  420.6 16.6 %reduce-scatter.33.cloned.1.call-done = bf16[2,512,3,64]{1,3,2,0:T(8,128)(2,1)} async-done(((bf16[2,2048,3,64]{1,3,2,0:T(8,128)(2,1)}), bf16[2,512,3,64]{1,3,2,0:T(8,128)(2,1)}) %reduce-scatter.33.cloned.1.call-update) | async-done | bytes 393232 | tf_op jit(solution)/shard_map/while/body/eval_jaxpr/reduce_scatter | solution.py:214
  450.1 36.3 %all-reduce.16.cloned.1.call-done = bf16[1024,768]{1,0:T(8,128)(2,1)} async-done(((bf16[1024,768]{1,0:T(8,128)(2,1)}), bf16[1024,768]{1,0:T(8,128)(2,1)}) %all-reduce.16.cloned.1.call-update) | async-done | bytes 1572880 | tf_op jit(solution)/shard_map/while/body/eval_jaxpr/psum | solution.py:86
  489.8 11.9 psum.128
  509.8 5.6 all_gather.86
  516.1 22.7 %all_gather.88 = bf16[768,3,192]{0,2,1:T(8,128)(2,1)} all-gather(bf16[384,3,192]{0,2,1:T(8,128)(2,1)} %get-tuple-element.776), channel_id=1, replica_groups=mesh['shard'=2,'ctx'=4,'tp'=4] {'shard'}, dimensions={0}, use_global_device_ids=true | all-gather | bytes 1327104 | tf_op jit(solution)/shard_map/while/body/eval_jaxpr/all_gather | solution.py:93
  544.9 12.2 all-gather.3
  557.1 5.9 all_gather.91
  566.0 12.5 all-gather.14.cloned.1.call-done
  580.5 11.1 fusion.198
  591.6 10.5 fusion.199
  602.1 14.3 %all-gather.12.cloned.1.call-done = bf16[2,2048,192]{1,0,2:T(2,128)(2,1)} async-done(((bf16[2,512,192]{1,0,2:T(2,128)(2,1)}), bf16[2,2048,192]{1,0,2:T(2,128)(2,1)}) %all-gather.12.cloned.1.call-update) | async-done | bytes 1572880 | tf_op jit(solution)/shard_map/while/body/eval_jaxpr/all_gather | solution.py:118
  618.5 11.1 fusion.200
  635.8 4.3 all_gather.93
  640.7 4.3 all_gather.94
  645.1 28.8 %all-reduce.10.cloned.1.call-done = bf16[1024,768]{1,0:T(8,128)(2,1)} async-done(((bf16[1024,768]{1,0:T(8,128)(2,1)}), bf16[1024,768]{1,0:T(8,128)(2,1)}) %all-reduce.10.cloned.1.call-update) | async-done | bytes 1572880 | tf_op jit(solution)/shard_map/while/body/eval_jaxpr/psum | solution.py:86
  677.3 20.8 %all-gather.16.cloned.1.call-done = bf16[768,768]{1,0:T(8,128)(2,1)} async-done(((bf16[384,768]{1,0:T(8,128)(2,1)}), bf16[768,768]{1,0:T(8,128)(2,1)}) %all-gather.16.cloned.1.call-update) | async-done | bytes 1179664 | tf_op jit(solution)/shard_map/while/body/eval_jaxpr/all_gather | solution.py:95
  698.1 5.1 multiply_convert_fusion.5
  703.2 19.1 %all-gather.18.cloned.1.call-done = bf16[768,768]{1,0:T(8,128)(2,1)} async-done(((bf16[384,768]{1,0:T(8,128)(2,1)}), bf16[768,768]{1,0:T(8,128)(2,1)}) %all-gather.18.cloned.1.call-update) | async-done | bytes 1179664 | tf_op jit(solution)/shard_map/while/body/eval_jaxpr/all_gather | solution.py:96
  722.3 4.3 convolution_convert_fusion.14
  730.2 39.5 %all-reduce.12.cloned.1.call-done = bf16[1024,768]{1,0:T(8,128)(2,1)} async-done(((bf16[1024,768]{1,0:T(8,128)(2,1)}), bf16[1024,768]{1,0:T(8,128)(2,1)}) %all-reduce.12.cloned.1.call-update) | async-done | bytes 1572880 | tf_op jit(solution)/shard_map/while/body/eval_jaxpr/psum | solution.py:86
  785.5 42.3 %all-reduce.14.cloned.1.call-done = bf16[1024,768]{1,0:T(8,128)(2,1)} async-done(((bf16[1024,768]{1,0:T(8,128)(2,1)}), bf16[1024,768]{1,0:T(8,128)(2,1)}) %all-reduce.14.cloned.1.call-update) | async-done | bytes 1572880 | tf_op jit(solution)/shard_map/while/body/eval_jaxpr/psum | solution.py:86
  835.8 11.7 fusion.206
  847.5 19.7 %multiply_reduce_fusion.13 = (f32[2,3,512]{2,1,0:T(4,128)S(1)}, f32[2,3,512,2048]{3,2,1,0:T(8,128)}) fusion(f32[2,3,512,2048]{3,2,1,0:T(8,128)} %get-tuple-element.679, f32[2,3,512]{2,1,0:T(4,128)S(1)} %log_add_fusion.2, bf16[2,2048,3,64]{1,3,2,0:T(8,128)(2,1)S(1)} %bitcast.245, bf16[2,512,3,64]{1,0,3,2:T(2,128)(2,1)S(1)} %reshape.329), kind=kOutput, calls=%fused_computation.1.clone.1 | convolution fusion | flops 824177664 | bytes 52322304 | tf_op jit(solution)/shard_map/while/body/eval_jaxpr/sqhd,skhd->shqk/dot_general | solution.py:194
  867.3 16.8 %multiply_convert_fusion.6 = bf16[2,3,512,2048]{3,2,1,0:T(8,128)(2,1)S(1)} fusion(f32[2,3,512,2048]{3,2,1,0:T(8,128)} %get-tuple-element.698, f32[2,3,512,2048]{3,2,1,0:T(8,128)} %get-tuple-element.679, f32[2,3,512]{2,1,0:T(4,128)S(1)} %get-tuple-element.699, f32[2,3,512]{2,1,0:T(4,128)S(1)} %log_add_fusion.2), kind=kLoop, calls=%fused_computation.clone.1 | loop fusion | flops 25165824 | bytes 62939136 | tf_op jit(solution)/shard_map/while/body/eval_jaxpr/convert_element_type | solution.py:198
  884.1 4.5 copy-done
  895.3 4.7 select_add_fusion.11
  900.1 4.8 select_add_fusion.10
  913.0 14.8 %reduce-scatter.33.cloned.1.call-done = bf16[2,512,3,64]{1,3,2,0:T(8,128)(2,1)} async-done(((bf16[2,2048,3,64]{1,3,2,0:T(8,128)(2,1)}), bf16[2,512,3,64]{1,3,2,0:T(8,128)(2,1)}) %reduce-scatter.33.cloned.1.call-update) | async-done | bytes 393232 | tf_op jit(solution)/shard_map/while/body/eval_jaxpr/reduce_scatter | solution.py:214
  943.2 33.8 %all-reduce.16.cloned.1.call-done = bf16[1024,768]{1,0:T(8,128)(2,1)} async-done(((bf16[1024,768]{1,0:T(8,128)(2,1)}), bf16[1024,768]{1,0:T(8,128)(2,1)}) %all-reduce.16.cloned.1.call-update) | async-done | bytes 1572880 | tf_op jit(solution)/shard_map/while/body/eval_jaxpr/psum | solution.py:86
  980.3 11.9 psum.128
  1016.9 7.9 reduce-scatter.27.cloned.1.call-done
  1026.7 11.7 reduce-scatter.17.cloned.1.call-done
  1038.4 14.8 %reduce-scatter.21.cloned.1.call-done = bf16[96,768]{1,0:T(8,128)(2,1)} async-done(((bf16[192,768]{1,0:T(8,128)(2,1)}), bf16[96,768]{1,0:T(8,128)(2,1)}) %reduce-scatter.21.cloned.1.call-update) | async-done | bytes 147472 | tf_op jit(solution)/shard_map/reduce_scatter | solution.py:297
  1053.2 24.6 %reduce-scatter.19.cloned.1.call-done = bf16[384,768]{1,0:T(8,128)(2,1)} async-done(((bf16[768,768]{1,0:T(8,128)(2,1)}), bf16[384,768]{1,0:T(8,128)(2,1)}) %reduce-scatter.19.cloned.1.call-update) | async-done | bytes 589840 | tf_op jit(solution)/shard_map/reduce_scatter | solution.py:291
  1077.8 24.6 %reduce-scatter.23.cloned.1.call-done = bf16[384,768]{1,0:T(8,128)(2,1)} async-done(((bf16[768,768]{1,0:T(8,128)(2,1)}), bf16[384,768]{1,0:T(8,128)(2,1)}) %reduce-scatter.23.cloned.1.call-update) | async-done | bytes 589840 | tf_op jit(solution)/shard_map/reduce_scatter | solution.py:300
  1102.4 24.6 %reduce-scatter.25.cloned.1.call-done = bf16[384,768]{1,0:T(8,128)(2,1)} async-done(((bf16[768,768]{1,0:T(8,128)(2,1)}), bf16[384,768]{1,0:T(8,128)(2,1)}) %reduce-scatter.25.cloned.1.call-update) | async-done | bytes 589840 | tf_op jit(solution)/shard_map/reduce_scatter | solution.py:303
  1127.1 13.1 %reduce-scatter.31.cloned.1.call-done = bf16[384,2]{1,0:T(8,128)(2,1)} async-done(((bf16[768,2]{1,0:T(8,128)(2,1)}), bf16[384,2]{1,0:T(8,128)(2,1)}) %reduce-scatter.31.cloned.1.call-update) | async-done | bytes 1552
  1141.1 12.1 reduce-scatter.29.cloned.1.call-done
  1154.2 11.9 all-reduce
  1167.3 87.1 %all-reduce.8.cloned.1.call-done = (bf16[64,768]{1,0:T(8,128)(2,1)}, bf16[384,768]{1,0:T(8,128)(2,1)}, bf16[384,3,192]{0,2,1:T(8,128)(2,1)}, bf16[96,768]{1,0:T(...) async-done(((bf16[64,768]{1,0:T(8,128)(2,1)}, bf16[384,768]{1,0:T(8,128)(2,1)}, bf16[384,3,192]{0,2,1:T(8,128)(2,1)}, bf16[96,768]{1,0:T(8,128)(2,1)}, ...) | async-done | bytes 2457616 | tf_op jit(solution)/shard_map/psum | solution.py:314
  (509 shorter events, 219.8 us)
Async XLA Ops:
  10.7 36.2 %copy-start.20 = (bf16[2,2,512,768]{3,2,1,0:T(8,128)(2,1)S(1)}, bf16[2,2,512,768]{3,2,1,0:T(8,128)(2,1)}, u32[]{:S(2)}) copy-start(bf16[2,2,512,768]{3,2,1,0:T(8,128)(2,1)} %get-tuple-element.773) | copy-start | bytes 9437188 | tf_op jit(solution)/shard_map/while
  10.7 34.6 %all-gather.10.cloned.1.call-start = ((), (), s32[]{:S(2)}) async-start(), calls=%async_computation.19 | async-start | bytes 1769472 | tf_op jit(solution)/shard_map/while/body/eval_jaxpr/all_gather | solution.py:92
  11.4 76.3 %all-gather.14.cloned.1.call-start = ((), (), s32[]{:S(2)}) async-start(), calls=%async_computation.21 | async-start | bytes 1966080 | tf_op jit(solution)/shard_map/while/body/eval_jaxpr/all_gather | solution.py:117
  48.4 14.2 %copy-start.30 = (bf16[96,768]{1,0:T(8,128)(2,1)S(1)}, bf16[96,768]{1,0:T(8,128)(2,1)}, u32[]{:S(2)}) copy-start(bf16[96,768]{1,0:T(8,128)(2,1)} %get-tuple-element.778) | copy-start | bytes 442372 | tf_op jit(solution)/shard_map/while
  49.6 76.3 %all-gather.12.cloned.1.call-start = ((), (), s32[]{:S(2)}) async-start(), calls=%async_computation.20 | async-start | bytes 1966080 | tf_op jit(solution)/shard_map/while/body/eval_jaxpr/all_gather | solution.py:118
  71.1 112.3 %all-reduce.10.cloned.1.call-start = ((), (), s32[]{:S(2)}) async-start(), calls=%async_computation.22 | async-start | bytes 3145728 | tf_op jit(solution)/shard_map/while/body/eval_jaxpr/psum | solution.py:86
  89.8 11.1 copy-start.8
  100.9 27.0 %copy-start.29 = (f32[2,3,512]{2,1,0:T(4,128)}, f32[2,3,512]{2,1,0:T(4,128)S(1)}, u32[]{:S(2)}) copy-start(f32[2,3,512]{2,1,0:T(4,128)S(1)} %get-tuple-element.680) | copy-start | bytes 36868 | tf_op jit(solution)/shard_map/while
  111.4 16.5 %copy-start.45 = (f32[2,3,512]{2,1,0:T(4,128)}, f32[2,3,512]{2,1,0:T(4,128)S(1)}, u32[]{:S(2)}) copy-start(f32[2,3,512]{2,1,0:T(4,128)S(1)} %fusion.199) | copy-start | bytes 36868 | tf_op jit(solution)/shard_map/while
  127.9 11.2 copy-start.11
  127.9 12.4 copy-start.22
  142.1 8.1 copy-start.61
  142.1 65.4 %all-gather.16.cloned.1.call-start = ((), (), s32[]{:S(2)}) async-start(), calls=%async_computation.23 | async-start | bytes 1769472 | tf_op jit(solution)/shard_map/while/body/eval_jaxpr/all_gather | solution.py:95
  142.7 89.0 %all-gather.18.cloned.1.call-start = ((), (), s32[]{:S(2)}) async-start(), calls=%async_computation.24 | async-start | bytes 1769472 | tf_op jit(solution)/shard_map/while/body/eval_jaxpr/all_gather | solution.py:96
  143.3 135.8 %all-reduce.12.cloned.1.call-start = ((), (), s32[]{:S(2)}) async-start(), calls=%async_computation.25 | async-start | bytes 3145728 | tf_op jit(solution)/shard_map/while/body/eval_jaxpr/psum | solution.py:86
  154.6 124.5 %copy-start.39 = (f32[768]{0:T(1024)}, f32[768]{0:T(1024)S(1)}, u32[]{:S(2)}) copy-start(f32[768]{0:T(1024)S(1)} %get-tuple-element.684) | copy-start | bytes 9220 | tf_op jit(solution)/shard_map/while
  186.2 155.1 %copy-start.1 = (f32[1024,768]{1,0:T(8,128)}, f32[1024,768]{1,0:T(8,128)S(1)}, u32[]{:S(2)}) copy-start(f32[1024,768]{1,0:T(8,128)S(1)} %get-tuple-element.681) | copy-start | bytes 9437188 | tf_op jit(solution)/shard_map/while
  186.2 92.9 %copy-start.31 = (f32[1024]{0:T(1024)}, f32[1024]{0:T(1024)S(1)}, u32[]{:S(2)}) copy-start(f32[1024]{0:T(1024)S(1)} %broadcast_multiply_fusion.9) | copy-start | bytes 12292 | tf_op jit(solution)/shard_map/while
  186.7 92.4 %copy-start.42 = (f32[1024]{0:T(1024)}, f32[1024]{0:T(1024)S(1)}, u32[]{:S(2)}) copy-start(f32[1024]{0:T(1024)S(1)} %add_rsqrt_fusion.4) | copy-start | bytes 12292 | tf_op jit(solution)/shard_map/while
  236.1 101.2 %all-reduce.14.cloned.1.call-start = ((), (), s32[]{:S(2)}) async-start(), calls=%async_computation.26 | async-start | bytes 3145728 | tf_op jit(solution)/shard_map/while/body/eval_jaxpr/psum | solution.py:86
  294.2 125.0 %reduce-scatter.35.cloned.1.call-start = ((), (), s32[]{:S(2)}) async-start(), calls=%async_computation.28 | async-start | bytes 1966080 | tf_op jit(solution)/shard_map/while/body/eval_jaxpr/reduce_scatter | solution.py:217
  345.2 11.8 copy-start.12
  357.0 80.3 %reduce-scatter.33.cloned.1.call-start = ((), (), s32[]{:S(2)}) async-start(), calls=%async_computation.27 | async-start | bytes 1966080 | tf_op jit(solution)/shard_map/while/body/eval_jaxpr/reduce_scatter | solution.py:214
  401.6 84.9 %all-reduce.16.cloned.1.call-start = ((), (), s32[]{:S(2)}) async-start(), calls=%async_computation.29 | async-start | bytes 3145728 | tf_op jit(solution)/shard_map/while/body/eval_jaxpr/psum | solution.py:86
  404.7 9.2 slice-start
  404.7 9.2 slice-start.1
  509.2 32.4 %copy-start.20 = (bf16[2,2,512,768]{3,2,1,0:T(8,128)(2,1)S(1)}, bf16[2,2,512,768]{3,2,1,0:T(8,128)(2,1)}, u32[]{:S(2)}) copy-start(bf16[2,2,512,768]{3,2,1,0:T(8,128)(2,1)} %get-tuple-element.773) | copy-start | bytes 9437188 | tf_op jit(solution)/shard_map/while
  509.2 30.7 %all-gather.10.cloned.1.call-start = ((), (), s32[]{:S(2)}) async-start(), calls=%async_computation.19 | async-start | bytes 1769472 | tf_op jit(solution)/shard_map/while/body/eval_jaxpr/all_gather | solution.py:92
  509.7 68.7 %all-gather.14.cloned.1.call-start = ((), (), s32[]{:S(2)}) async-start(), calls=%async_computation.21 | async-start | bytes 1966080 | tf_op jit(solution)/shard_map/while/body/eval_jaxpr/all_gather | solution.py:117
  543.0 14.1 %copy-start.30 = (bf16[96,768]{1,0:T(8,128)(2,1)S(1)}, bf16[96,768]{1,0:T(8,128)(2,1)}, u32[]{:S(2)}) copy-start(bf16[96,768]{1,0:T(8,128)(2,1)} %get-tuple-element.778) | copy-start | bytes 442372 | tf_op jit(solution)/shard_map/while
  544.2 72.2 %all-gather.12.cloned.1.call-start = ((), (), s32[]{:S(2)}) async-start(), calls=%async_computation.20 | async-start | bytes 1966080 | tf_op jit(solution)/shard_map/while/body/eval_jaxpr/all_gather | solution.py:118
  565.6 108.3 %all-reduce.10.cloned.1.call-start = ((), (), s32[]{:S(2)}) async-start(), calls=%async_computation.22 | async-start | bytes 3145728 | tf_op jit(solution)/shard_map/while/body/eval_jaxpr/psum | solution.py:86
  580.5 11.1 copy-start.8
  591.6 26.9 %copy-start.29 = (f32[2,3,512]{2,1,0:T(4,128)}, f32[2,3,512]{2,1,0:T(4,128)S(1)}, u32[]{:S(2)}) copy-start(f32[2,3,512]{2,1,0:T(4,128)S(1)} %get-tuple-element.680) | copy-start | bytes 36868 | tf_op jit(solution)/shard_map/while
  602.1 16.4 %copy-start.45 = (f32[2,3,512]{2,1,0:T(4,128)}, f32[2,3,512]{2,1,0:T(4,128)S(1)}, u32[]{:S(2)}) copy-start(f32[2,3,512]{2,1,0:T(4,128)S(1)} %fusion.199) | copy-start | bytes 36868 | tf_op jit(solution)/shard_map/while
  618.4 11.2 copy-start.11
  618.5 12.4 copy-start.22
  632.7 8.1 copy-start.61
  632.7 65.5 %all-gather.16.cloned.1.call-start = ((), (), s32[]{:S(2)}) async-start(), calls=%async_computation.23 | async-start | bytes 1769472 | tf_op jit(solution)/shard_map/while/body/eval_jaxpr/all_gather | solution.py:95
  633.3 89.0 %all-gather.18.cloned.1.call-start = ((), (), s32[]{:S(2)}) async-start(), calls=%async_computation.24 | async-start | bytes 1769472 | tf_op jit(solution)/shard_map/while/body/eval_jaxpr/all_gather | solution.py:96
  633.8 135.8 %all-reduce.12.cloned.1.call-start = ((), (), s32[]{:S(2)}) async-start(), calls=%async_computation.25 | async-start | bytes 3145728 | tf_op jit(solution)/shard_map/while/body/eval_jaxpr/psum | solution.py:86
  645.1 124.5 %copy-start.39 = (f32[768]{0:T(1024)}, f32[768]{0:T(1024)S(1)}, u32[]{:S(2)}) copy-start(f32[768]{0:T(1024)S(1)} %get-tuple-element.684) | copy-start | bytes 9220 | tf_op jit(solution)/shard_map/while
  676.8 155.1 %copy-start.1 = (f32[1024,768]{1,0:T(8,128)}, f32[1024,768]{1,0:T(8,128)S(1)}, u32[]{:S(2)}) copy-start(f32[1024,768]{1,0:T(8,128)S(1)} %get-tuple-element.681) | copy-start | bytes 9437188 | tf_op jit(solution)/shard_map/while
  676.8 92.9 %copy-start.31 = (f32[1024]{0:T(1024)}, f32[1024]{0:T(1024)S(1)}, u32[]{:S(2)}) copy-start(f32[1024]{0:T(1024)S(1)} %broadcast_multiply_fusion.9) | copy-start | bytes 12292 | tf_op jit(solution)/shard_map/while
  677.3 92.4 %copy-start.42 = (f32[1024]{0:T(1024)}, f32[1024]{0:T(1024)S(1)}, u32[]{:S(2)}) copy-start(f32[1024]{0:T(1024)S(1)} %add_rsqrt_fusion.4) | copy-start | bytes 12292 | tf_op jit(solution)/shard_map/while
  726.6 101.2 %all-reduce.14.cloned.1.call-start = ((), (), s32[]{:S(2)}) async-start(), calls=%async_computation.26 | async-start | bytes 3145728 | tf_op jit(solution)/shard_map/while/body/eval_jaxpr/psum | solution.py:86
  784.7 126.8 %reduce-scatter.35.cloned.1.call-start = ((), (), s32[]{:S(2)}) async-start(), calls=%async_computation.28 | async-start | bytes 1966080 | tf_op jit(solution)/shard_map/while/body/eval_jaxpr/reduce_scatter | solution.py:217
  835.7 11.8 copy-start.12
  847.5 80.3 %reduce-scatter.33.cloned.1.call-start = ((), (), s32[]{:S(2)}) async-start(), calls=%async_computation.27 | async-start | bytes 1966080 | tf_op jit(solution)/shard_map/while/body/eval_jaxpr/reduce_scatter | solution.py:214
  892.1 84.9 %all-reduce.16.cloned.1.call-start = ((), (), s32[]{:S(2)}) async-start(), calls=%async_computation.29 | async-start | bytes 3145728 | tf_op jit(solution)/shard_map/while/body/eval_jaxpr/psum | solution.py:86
  895.3 11.0 slice-start
  895.3 11.0 slice-start.1
  1002.8 22.0 %reduce-scatter.27.cloned.1.call-start = ((), (), s32[]{:S(2)}) async-start(), calls=%async_computation.15 | async-start | bytes 1474560
  1002.8 6.6 copy-start.19
  1007.7 30.7 %reduce-scatter.17.cloned.1.call-start = ((), (), s32[]{:S(2)}) async-start(), calls=%async_computation.10 | async-start | bytes 294912 | tf_op jit(solution)/shard_map/reduce_scatter | solution.py:288
  1008.5 44.6 %reduce-scatter.21.cloned.1.call-start = ((), (), s32[]{:S(2)}) async-start(), calls=%async_computation.12 | async-start | bytes 442368 | tf_op jit(solution)/shard_map/reduce_scatter | solution.py:297
  1009.4 68.4 %reduce-scatter.19.cloned.1.call-start = ((), (), s32[]{:S(2)}) async-start(), calls=%async_computation.11 | async-start | bytes 1769472 | tf_op jit(solution)/shard_map/reduce_scatter | solution.py:291
  1010.6 91.8 %reduce-scatter.23.cloned.1.call-start = ((), (), s32[]{:S(2)}) async-start(), calls=%async_computation.13 | async-start | bytes 1769472 | tf_op jit(solution)/shard_map/reduce_scatter | solution.py:300
  1013.7 113.4 %reduce-scatter.25.cloned.1.call-start = ((), (), s32[]{:S(2)}) async-start(), calls=%async_computation.14 | async-start | bytes 1769472 | tf_op jit(solution)/shard_map/reduce_scatter | solution.py:303
  1014.9 125.3 %reduce-scatter.31.cloned.1.call-start = ((), (), s32[]{:S(2)}) async-start(), calls=%async_computation.17 | async-start | bytes 294912
  1015.9 137.4 %reduce-scatter.29.cloned.1.call-start = ((), (), s32[]{:S(2)}) async-start(), calls=%async_computation.16 | async-start | bytes 294912
  1016.8 237.6 %all-reduce.8.cloned.1.call-start = ((), (), s32[]{:S(2)}) async-start(), calls=%async_computation.18 | async-start | bytes 4915200 | tf_op jit(solution)/shard_map/psum | solution.py:314
  1254.4 7.5 copy-start.48
  1254.4 8.6 copy-start.47
  (101 other events, 332.5 us)
Sparse Core Ops, SparseCore 0:
  13.1 32.2 all-gather.9
  49.7 38.0 all-gather.13
  89.9 35.8 all-gather.11
  142.2 41.0 all-reduce.9
  184.7 22.7 all-gather.15
  209.0 22.7 all-gather.17
  236.2 42.8 all-reduce.11
  294.3 42.8 all-reduce.13
  357.1 35.4 reduce-scatter.34
  401.7 35.5 reduce-scatter.32
  444.7 41.7 all-reduce.15
  511.2 28.6 all-gather.9
  544.3 34.1 all-gather.13
  580.5 35.8 all-gather.11
  632.8 41.0 all-reduce.9
  675.3 22.7 all-gather.15
  699.5 22.7 all-gather.17
  726.7 42.8 all-reduce.11
  784.8 42.8 all-reduce.13
  847.6 35.4 reduce-scatter.34
  892.2 35.5 reduce-scatter.32
  935.2 41.7 all-reduce.15
Sparse Core Ops, SparseCore 1:
  1007.8 16.9 reduce-scatter.26
  1027.4 10.9 reduce-scatter.16
  1041.1 12.0 reduce-scatter.20
  1056.0 21.7 reduce-scatter.18
  1080.6 21.7 reduce-scatter.22
  1105.3 21.7 reduce-scatter.24
  1129.2 10.9 reduce-scatter.30
  1142.3 10.9 reduce-scatter.28
  1156.5 97.8 all-reduce.7
where the time goes:
time: 1270 us
  waiting for transfers between devices  688 us (54%)
  matrix products  205 us (16%)
  blocking collectives  147 us (12%)
  other arithmetic  131 us (10%)
  local copies, waits for them, and re-layouts  77.3 us (6%)
  between operations  16.3 us (1%)
    psum x8, waiting for transfers between devices, summed(): lax.psum(terms_fn(0, rows).astype(jnp.bfloat16), 'tp').astype(jnp.float32)  291 us
    psum x1, waiting for transfers between devices, body(): lax.psum(pieces[0].astype(jnp.bfloat16), 'ctx').astype(jnp.float32)  87.1 us
    all_gather x2, blocking collectives, step(): lax.all_gather(local_weights[2], 'shard', axis=0, tiled=True)  44.9 us
    all_gather x2, waiting for transfers between devices, step(): lax.all_gather(local_weights[4], 'shard', axis=0, tiled=True)  41.7 us
    dot_general x2, matrix products, step(): jnp.einsum('sqhd,skhd->shqk', grad_attended, values_all, preferred_elemen...  39.5 us
    all_gather x2, waiting for transfers between devices, step(): lax.all_gather(local_weights[5], 'shard', axis=0, tiled=True)  38.2 us
    dot_general x12, matrix products, inner_rows(): lax.dot_general(left, right, (((0,), (0,)), ((), ())), preferred_element_...  35.1 us
    convert_element_type x2, other arithmetic, step(): grad_scores = (probs_again * (grad_probs - centre)).astype(jnp.bfloat16)  33.6 us
  transfers between devices with their start and end apart: 31, of which 29 were waited for; matrix products, arithmetic and copies ran while one was open for 18% of the time, Pallas kernels for 0%

commit v1 on v0

v1 whole, which is shorter than its diff:
```python
import functools
import math

import jax
import jax.numpy as jnp
from jax import lax
from jax.experimental import pallas as pl
from jax.experimental.pallas import tpu as pltpu
from jax.sharding import PartitionSpec as P

HEAD_DIM = 64
NORM_EPS = 1e-05
BIG = 1e30
BF = jnp.bfloat16
F32 = jnp.float32
MESH = pl.DeviceIdType.MESH


def time_features(steps_in, width):
    half = width // 2
    ratios = jnp.exp(-math.log(10000.0) * jnp.arange(half, dtype=F32) / half)
    angles = steps_in.astype(F32)[:, None] * ratios[None, :]
    return jnp.concatenate([jnp.cos(angles), jnp.sin(angles)], axis=1)


def silu_fn(value):
    return value / (1.0 + jnp.exp(-value))


def gelu_pair(v):
    half = 0.5 * (1.0 + lax.erf(v * (1.0 / math.sqrt(2.0))))
    bell = jnp.exp(-0.5 * v * v) * (1.0 / math.sqrt(2.0 * math.pi))
    return v * half, half + v * bell


def contract(left, right, ldim, rdim):
    return lax.dot_general(left, right, (((ldim,), (rdim,)), ((), ())), preferred_element_type=F32)


def dot(a, b):
    return contract(a, b, 1, 0)


def send(src, dst, send_sem, recv_sem, **where):
    return pltpu.make_async_remote_copy(
        src_ref=src, dst_ref=dst, send_sem=send_sem, recv_sem=recv_sem,
        device_id=where, device_id_type=MESH,
    )


def meet(peers):
    barrier = pltpu.get_barrier_semaphore()
    for where in peers:
        pl.semaphore_signal(barrier, inc=1, device_id=where, device_id_type=MESH)
    pl.semaphore_wait(barrier, len(peers))


def attend_kernel(heads, bk, lo_ref, hi_ref, qt_ref, kv_ref, aq_ref, ak_ref, ot_ref, lse_ref, ka, vat):
    i = pl.program_id(0)
    hd = qt_ref.shape[0] // heads
    parts, _, piece = ot_ref.shape
    each = range(heads)

    @pl.when(i == 0)
    def _():
        for h in each:
            ka[h] = jnp.concatenate([kv_ref[h * hd : (h + 1) * hd], ak_ref[...]], axis=0).T
            vat[h] = jnp.concatenate([kv_ref[(heads + h) * hd : (heads + h + 1) * hd], ak_ref[:16, :]], axis=0)

    bq = qt_ref.shape[1]
    qa = [jnp.concatenate([qt_ref[h * hd : (h + 1) * hd], aq_ref[...]], axis=0) for h in each]

    def step(j, carry):
        off = pl.multiple_of(j * bk, bk)
        s = [dot(ka[h, pl.ds(off, bk), :], qa[h]) for h in each]
        out = []
        for h in each:
            m, acc = carry[h]
            mn = jnp.maximum(m, jnp.max(s[h], axis=0, keepdims=True))
            p = jnp.exp(s[h] - mn).astype(BF)
            out.append((mn, acc * jnp.exp(m - mn) + dot(vat[h, :, pl.ds(off, bk)], p)))
        return tuple(out)

    m0 = jnp.full((1, bq), -BIG * 2, F32)
    a0 = jnp.zeros((hd + 16, bq), F32)
    done = lax.fori_loop(lo_ref[i], hi_ref[i], step, ((m0, a0),) * heads)
    for h in each:
        m, acc = done[h]
        total = acc[hd + 4 : hd + 5, :]
        out = (acc[:hd, :] / total).astype(BF)
        for t in range(parts):
            ot_ref[t, h * hd : (h + 1) * hd, :] = out[:, t * piece : (t + 1) * piece]
        lse_ref[h] = m + jnp.log(total)


def attend(joint_t, aq, ak, lo, hi, heads, hd, parts, bq, bk):
    n = joint_t.shape[1]
    w = heads * hd
    piece = bq // parts
    return pl.pallas_call(
        functools.partial(attend_kernel, heads, bk),
        out_shape=(
            jax.ShapeDtypeStruct((parts, w, n // parts), BF),
            jax.ShapeDtypeStruct((heads, 1, n), F32),
        ),
        grid_spec=pltpu.PrefetchScalarGridSpec(
            num_scalar_prefetch=2,
            grid=(n // bq,),
            in_specs=[
                pl.BlockSpec((w, bq), lambda i, *_: (0, i)),
                pl.BlockSpec((2 * w, n), lambda i, *_: (0, 0)),
                pl.BlockSpec((64, bq), lambda i, *_: (0, i)),
                pl.BlockSpec((64, n), lambda i, *_: (0, 0)),
            ],
            out_specs=[
                pl.BlockSpec((parts, w, piece), lambda i, *_: (0, 0, i)),
                pl.BlockSpec((heads, 1, bq), lambda i, *_: (0, 0, i)),
            ],
            scratch_shapes=[
                pltpu.VMEM((heads, n, hd + 64), BF),
                pltpu.VMEM((heads, hd + 16, n), BF),
            ],
        ),
        name="attend",
        cost_estimate=pl.CostEstimate(
            flops=4 * heads * n * n * hd, bytes_accessed=8 * heads * n * hd, transcendentals=heads * n * n
        ),
    )(lo, hi, joint_t[:w], joint_t[w:], aq, ak)


def split3(v):
    a = v.astype(BF)
    r = v - a.astype(F32)
    b = r.astype(BF)
    c = (r - b.astype(F32)).astype(BF)
    return a, b, c


def attend_back_kernel(
    heads, bk, scale, lo_ref, hi_ref, qt_ref, kv_ref, aq_ref, ak_ref, ot_ref, gt_ref, lse_ref,
    dq_ref, dkv_ref, ka, va, acc,
):
    i = pl.program_id(0)
    w, bq = qt_ref.shape
    parts = ot_ref.shape[0]
    hd = w // heads
    each = range(heads)

    @pl.when(i == 0)
    def _():
        for h in each:
            ka[h] = jnp.concatenate([kv_ref[h * hd : (h + 1) * hd], ak_ref[...]], axis=0).T
            va[h] = jnp.concatenate([kv_ref[(heads + h) * hd : (heads + h + 1) * hd], ak_ref[...]], axis=0).T
        acc[...] = jnp.zeros_like(acc)

    row = lax.broadcasted_iota(jnp.int32, (64, bq), 0)

    def rows3(v):
        a, b, c = split3(v)
        return (
            jnp.where(row == 4, a.astype(F32), 0.0)
            + jnp.where(row == 5, b.astype(F32), 0.0)
            + jnp.where(row == 6, c.astype(F32), 0.0)
        )

    qa, ga, right = [], [], []
    for h in each:
        part = slice(h * hd, (h + 1) * hd)
        qt = qt_ref[part]
        gt = jnp.concatenate([gt_ref[t, part, :] for t in range(parts)], axis=1)
        ot = jnp.concatenate([ot_ref[t, part, :] for t in range(parts)], axis=1)
        delta = jnp.sum(gt.astype(F32) * ot.astype(F32), axis=0, keepdims=True)
        qa.append(jnp.concatenate([qt, (aq_ref[...].astype(F32) + rows3(-lse_ref[h])).astype(BF)], axis=0))
        ga.append(jnp.concatenate([gt, rows3(-delta).astype(BF)], axis=0))
        zero = jnp.zeros_like(qt)
        right.append(
            jnp.concatenate(
                [jnp.concatenate([qt, zero], axis=0).T, jnp.concatenate([zero, gt], axis=0).T], axis=0
            )
        )

    def step(j, dq):
        off = pl.multiple_of(j * bk, bk)
        s = [dot(ka[h, pl.ds(off, bk), :], qa[h]) for h in each]
        g = [dot(va[h, pl.ds(off, bk), :], ga[h]) for h in each]
        out = []
        for h in each:
            p = jnp.exp(s[h])
            ds = (p * g[h]).astype(BF)
            acc[h, pl.ds(off, bk), :] += dot(jnp.concatenate([ds, p.astype(BF)], axis=1), right[h])
            out.append(dq[h] + dot(kv_ref[h * hd : (h + 1) * hd, pl.ds(off, bk)], ds))
        return tuple(out)

    dq = lax.fori_loop(lo_ref[i], hi_ref[i], step, (jnp.zeros((hd, bq), F32),) * heads)
    for h in each:
        dq_ref[h * hd : (h + 1) * hd] = (dq[h] * scale).astype(BF)

    @pl.when(i == pl.num_programs(0) - 1)
    def _():
        for h in each:
            full = acc[h].T
            dkv_ref[h * hd : (h + 1) * hd] = full[:hd].astype(BF)
            dkv_ref[(heads + h) * hd : (heads + h + 1) * hd] = full[hd:].astype(BF)


def attend_back(joint_t, aq, ak, ot, got, lse, lo, hi, heads, hd, parts, bq, bk):
    n = joint_t.shape[1]
    w = heads * hd
    piece = bq // parts
    return pl.pallas_call(
        functools.partial(attend_back_kernel, heads, bk, hd ** -0.5),
        out_shape=(jax.ShapeDtypeStruct((w, n), BF), jax.ShapeDtypeStruct((2 * w, n), BF)),
        grid_spec=pltpu.PrefetchScalarGridSpec(
            num_scalar_prefetch=2,
            grid=(n // bq,),
            in_specs=[
                pl.BlockSpec((w, bq), lambda i, *_: (0, i)),
                pl.BlockSpec((2 * w, n), lambda i, *_: (0, 0)),
                pl.BlockSpec((64, bq), lambda i, *_: (0, i)),
                pl.BlockSpec((64, n), lambda i, *_: (0, 0)),
                pl.BlockSpec((parts, w, piece), lambda i, *_: (0, 0, i)),
                pl.BlockSpec((parts, w, piece), lambda i, *_: (0, 0, i)),
                pl.BlockSpec((heads, 1, bq), lambda i, *_: (0, 0, i)),
            ],
            out_specs=[
                pl.BlockSpec((w, bq), lambda i, *_: (0, i)),
                pl.BlockSpec((2 * w, n), lambda i, *_: (0, 0)),
            ],
            scratch_shapes=[
                pltpu.VMEM((heads, n, hd + 64), BF),
                pltpu.VMEM((heads, n, hd + 64), BF),
                pltpu.VMEM((heads, n, 2 * hd), F32),
            ],
        ),
        name="attend_back",
        cost_estimate=pl.CostEstimate(
            flops=10 * heads * n * n * hd, bytes_accessed=16 * heads * n * hd, transcendentals=heads * n * n
        ),
    )(lo, hi, joint_t[:w], joint_t[w:], aq, ak, ot, got, lse)


def mask_rows(seg):
    n = seg.shape[0]
    one = seg[None, :] == jnp.arange(4, dtype=jnp.int32)[:, None]
    aq = jnp.concatenate([jnp.where(one, 0.0, -BIG).astype(BF), jnp.zeros((60, n), BF)], axis=0)
    ak = jnp.concatenate([one.astype(BF), jnp.ones((3, n), BF), jnp.zeros((57, n), BF)], axis=0)
    return aq, ak


def key_ranges(seg, bq, bk):
    first = seg[::bq]
    last = seg[bq - 1 :: bq]
    lo = jnp.sum(seg[None, :] < first[:, None], axis=1) // bk
    hi = (jnp.sum(seg[None, :] <= last[:, None], axis=1) + bk - 1) // bk
    return lo.astype(jnp.int32), hi.astype(jnp.int32)


def spread_kernel(extras, src, *refs):
    ins, dst, outs = refs[:extras], refs[extras], refs[extras + 1 : 2 * extras + 1]
    loc, zs, zr, ys, yr, cs, cr, es, er = refs[2 * extras + 1 :]
    z, q = lax.axis_index("ctx"), lax.axis_index("tp")
    count = lax.axis_size("ctx")
    wide = extras > 0
    rows = dst.shape[1] // lax.axis_size("tp")
    mine = pl.ds(pl.multiple_of(q * rows, rows), rows)
    far = q ^ 2
    far_rows = pl.ds(pl.multiple_of(far * rows, rows), rows)
    meet([{"ctx": lax.rem(z + d, count)} for d in range(1, count)] + [{"tp": q ^ 1}, {"tp": q ^ 2}])

    def hop(d):
        to = lax.rem(z + d, count)
        block = src.at[to, mine] if wide else src.at[to]
        return send(block, dst.at[z, mine], zs.at[d], zr.at[d], ctx=to)

    def part(ref, out, c):
        return ref.at[c] if ref.shape == out.shape else ref.at[c, mine]

    def hop_extra(e, d):
        to = lax.rem(z + d, count)
        return send(part(ins[e], outs[e], to), outs[e].at[z], es.at[e, d], er.at[e, d], ctx=to)

    for d in range(1, count):
        hop(d).start()
    if wide:
        keep = [pltpu.make_async_copy(src.at[z], dst.at[z], loc.at[0])]
        for e in range(extras):
            keep.append(pltpu.make_async_copy(part(ins[e], outs[e], z), outs[e].at[z], loc.at[e + 1]))
        for copy in keep:
            copy.start()
        for e in range(extras):
            for d in range(1, count):
                hop_extra(e, d).start()
        order = list(range(1, count))
    else:
        own = pltpu.make_async_copy(src.at[z], dst.at[z, mine], loc.at[0])
        own.start()
        own.wait()
        keep = []
        order = list(range(count))

    def across(d):
        at = dst.at[lax.rem(z + count - d, count), mine]
        return send(at, at, ys.at[d], yr.at[d], tp=far)

    def across_in(d):
        at = dst.at[lax.rem(z + count - d, count), far_rows]
        return send(at, at, ys.at[d], yr.at[d], tp=far)

    def beside(d, second):
        at = dst.at[lax.rem(z + count - d, count), far_rows if second else mine]
        return send(at, at, cs.at[second, d], cr.at[second, d], tp=q ^ 1)

    for d in order:
        if d:
            hop(d).wait_recv()
        across(d).start()
        beside(d, 0).start()
    for d in order:
        across_in(d).wait_recv()
        beside(d, 1).start()
    for d in order:
        if d:
            hop(d).wait_send()
        across(d).wait_send()
        for second in (0, 1):
            beside(d, second).wait()
    for copy in keep:
        copy.wait()
    for e in range(extras):
        for d in range(1, count):
            hop_extra(e, d).wait()


def spread(src, extras, out_rows, extra_shapes, ident):
    count, _, width = src.shape
    sem = pltpu.SemaphoreType.DMA
    n = max(len(extras), 1)
    shapes = [jax.ShapeDtypeStruct((count, out_rows, width), src.dtype)]
    shapes += [jax.ShapeDtypeStruct(shape, x.dtype) for shape, x in zip(extra_shapes, extras)]
    return pl.pallas_call(
        functools.partial(spread_kernel, len(extras)),
        out_shape=shapes,
        in_specs=[pl.BlockSpec(memory_space=pltpu.VMEM)] * (1 + len(extras)),
        out_specs=[pl.BlockSpec(memory_space=pltpu.VMEM)] * (1 + len(extras)),
        scratch_shapes=[sem((1 + n,)), sem((count,)), sem((count,)), sem((count,)), sem((count,)),
                        sem((2, count)), sem((2, count)), sem((n, count)), sem((n, count))],
        compiler_params=pltpu.CompilerParams(collective_id=ident, has_side_effects=True),
        name="spread",
    )(src, *extras)


def swap_kernel(src_abs, dst_abs, src, dst, ss, rs, loc):
    q = lax.axis_index("tp")
    count = lax.axis_size("tp")
    meet([{"tp": q ^ r} for r in range(1, count)])

    def hop(r):
        return send(src.at[q ^ r if src_abs else r], dst.at[q if dst_abs else r], ss.at[r], rs.at[r], tp=q ^ r)

    for r in range(count - 1, 0, -1):
        hop(r).start()
    own = pltpu.make_async_copy(src.at[q if src_abs else 0], dst.at[q if dst_abs else 0], loc.at[0])
    own.start()
    own.wait()
    for r in range(1, count):
        hop(r).wait()


def swap(x, src_abs, dst_abs, ident):
    sem = pltpu.SemaphoreType.DMA
    count = x.shape[0]
    return pl.pallas_call(
        functools.partial(swap_kernel, src_abs, dst_abs),
        out_shape=jax.ShapeDtypeStruct(x.shape, x.dtype),
        in_specs=[pl.BlockSpec(memory_space=pltpu.VMEM)],
        out_specs=pl.BlockSpec(memory_space=pltpu.VMEM),
        scratch_shapes=[sem((count,)), sem((count,)), sem((1,))],
        compiler_params=pltpu.CompilerParams(collective_id=ident, has_side_effects=True),
        name="swap",
    )(x)


def fold_kernel(terms, out, near, relay, away, s1, r1, s2, r2):
    q = lax.axis_index("tp")
    count, _, _ = out.shape
    rows = out.shape[1]

    def quarter(p):
        return pl.ds(pl.multiple_of(p * rows, rows), rows)

    meet([{"tp": q ^ 1}, {"tp": q ^ 2}])

    def first(c, k):
        return send(terms.at[c, quarter(q ^ (3 if k else 1))], near.at[k, c], s1.at[k, c], r1.at[k, c], tp=q ^ 1)

    def second(c):
        return send(relay.at[c], away.at[c], s2.at[c], r2.at[c], tp=q ^ 2)

    for k in (1, 0):
        for c in range(count):
            first(c, k).start()
    for c in range(count):
        first(c, 1).wait_recv()
        relay[c] = (terms[c, quarter(q ^ 2), :].astype(F32) + near[1, c].astype(F32)).astype(BF)
        second(c).start()
    for c in range(count):
        first(c, 0).wait_recv()
        second(c).wait_recv()
        out[c] = terms[c, quarter(q), :].astype(F32) + near[0, c].astype(F32) + away[c].astype(F32)
    for c in range(count):
        first(c, 0).wait_send()
        first(c, 1).wait_send()
        second(c).wait_send()


def fold(terms, ident):
    count, n, width = terms.shape
    rows = n // lax.axis_size("tp")
    sem = pltpu.SemaphoreType.DMA
    return pl.pallas_call(
        fold_kernel,
        out_shape=jax.ShapeDtypeStruct((count, rows, width), F32),
        in_specs=[pl.BlockSpec(memory_space=pltpu.VMEM)],
        out_specs=pl.BlockSpec(memory_space=pltpu.VMEM),
        scratch_shapes=[pltpu.VMEM((2, count, rows, width), BF), pltpu.VMEM((count, rows, width), BF),
                        pltpu.VMEM((count, rows, width), BF), sem((2, count)), sem((2, count)), sem((count,)), sem((count,))],
        compiler_params=pltpu.CompilerParams(collective_id=ident, has_side_effects=True),
        name="fold",
    )(terms)


def norm(rows):
    mean = jnp.mean(rows, axis=-1, keepdims=True)
    centred = rows - mean
    inverse = lax.rsqrt(jnp.mean(centred * centred, axis=-1, keepdims=True) + NORM_EPS)
    return centred * inverse, inverse


def norm_back(grad, normed, inverse, gain):
    scaled = grad * gain
    return inverse * (
        scaled
        - jnp.mean(scaled, axis=-1, keepdims=True)
        - normed * jnp.mean(scaled * normed, axis=-1, keepdims=True)
    )


def middle_kernel(
    chunk, att, tok, te, affine, cot, w_out, w_in, w_down,
    out, gjs, gatt, g_out, g_in, g_down, sums, fl, sl, bl, act, gi, gp,
):
    slots = w_in.shape[0]
    n, width = tok.shape
    sums[...] = jnp.zeros_like(sums)

    def rows_step(j, carry):
        rows = pl.ds(pl.multiple_of(j * chunk, chunk), chunk)
        gain1, shift1 = affine[0:1, :], affine[1:2, :]
        gain2, shift2 = affine[2:3, :], affine[3:4, :]
        branch = contract(att[:, rows], w_out[...], 0, 0)
        normed1, inverse1 = norm(tok[rows, :].astype(F32) + te[...] + branch)
        first = normed1 * gain1 + shift1
        fl[rows, :] = first.astype(BF)
        second = first
        for t in range(slots):
            up, slope = gelu_pair(dot(fl[rows, :], w_in[t]))
            gp[t] = slope
            act[t, rows, :] = up.astype(BF)
            second += dot(act[t, rows, :], w_down[t])
        normed2, inverse2 = norm(second)
        out[rows, :] = (normed2 * gain2 + shift2).astype(BF)
        grad = cot[rows, :].astype(F32)
        sums[2:3, :] += jnp.sum(grad * normed2, axis=0, keepdims=True)
        sums[3:4, :] += jnp.sum(grad, axis=0, keepdims=True)
        grad = norm_back(grad, normed2, inverse2, gain2)
        sl[rows, :] = grad.astype(BF)
        for t in range(slots):
            gi[t, rows, :] = (contract(sl[rows, :], w_down[t], 1, 1) * gp[t]).astype(BF)
            grad += contract(gi[t, rows, :], w_in[t], 1, 1)
        sums[0:1, :] += jnp.sum(grad * normed1, axis=0, keepdims=True)
        sums[1:2, :] += jnp.sum(grad, axis=0, keepdims=True)
        grad = norm_back(grad, normed1, inverse1, gain1)
        gjs[rows, :] = grad
        bl[rows, :] = grad.astype(BF)
        gatt[:, rows] = contract(w_out[...], bl[rows, :], 1, 1).astype(BF)
        return carry

    lax.fori_loop(0, n // chunk, rows_step, 0)
    block = 256

    def slot_step(t, carry):
        for b in range(width // block):
            part = slice(b * block, (b + 1) * block)
            g_in[t, part, :] = contract(fl[:, part], gi[t], 0, 0).astype(BF)
        for b in range(w_down.shape[1] // block):
            part = slice(b * block, (b + 1) * block)
            g_down[t, part, :] = contract(act[t, :, part], sl[...], 0, 0).astype(BF)
        return carry

    lax.fori_loop(0, slots, slot_step, 0)
    for b in range(att.shape[0] // block):
        part = slice(b * block, (b + 1) * block)
        g_out[part, :] = dot(att[part, :], bl[...]).astype(BF)


def middle(att, tok, te, affine, cot, w_out, w_in, w_down, chunk=256):
    n, width = tok.shape
    slots, _, units = w_in.shape
    shape = jax.ShapeDtypeStruct
    vmem = pl.BlockSpec(memory_space=pltpu.VMEM)
    return pl.pallas_call(
        functools.partial(middle_kernel, chunk),
        out_shape=(
            shape((n, width), BF), shape((n, width), F32), shape(att.shape, BF),
            shape(w_out.shape, BF), shape(w_in.shape, BF), shape(w_down.shape, BF), shape((8, width), F32),
        ),
        in_specs=[vmem] * 8,
        out_specs=[vmem] * 7,
        scratch_shapes=[
            pltpu.VMEM((n, width), BF), pltpu.VMEM((n, width), BF), pltpu.VMEM((n, width), BF),
            pltpu.VMEM((slots, n, units), BF), pltpu.VMEM((slots, n, units), BF), pltpu.VMEM((slots, chunk, units), F32),
        ],
        name="middle",
        cost_estimate=pl.CostEstimate(
            flops=12 * n * width * (slots * units + width // 2), bytes_accessed=24 * slots * width * units, transcendentals=2 * n * slots * units
        ),
    )(att, tok, te, affine, cot, w_out, w_in, w_down)


def body(
    tokens, segments, timesteps, w_time1, w_time2, w_qkv, w_out, w_in, w_down, norm_gains, norm_shifts, cotangent
):
    seqs, length, width = tokens.shape
    shards, ctx, tp = lax.axis_size("shard"), lax.axis_size("ctx"), lax.axis_size("tp")
    x, z, q = lax.axis_index("shard"), lax.axis_index("ctx"), lax.axis_index("tp")
    if seqs != ctx or tp != 4:
        raise ValueError("unsupported mesh")
    rows = length // tp
    full = ctx * length
    heads = w_qkv.shape[2] // HEAD_DIM
    local = heads * HEAD_DIM

    def shard_gather(v):
        if shards == 2:
            other = lax.ppermute(v, "shard", [(0, 1), (1, 0)])
            return jnp.where(x == 0, jnp.stack([v, other]), jnp.stack([other, v]))
        return lax.all_gather(v, "shard", axis=0)

    def shard_sum(v):
        if shards == 2:
            return v + lax.ppermute(v, "shard", [(0, 1), (1, 0)])
        return lax.psum(v, "shard")

    def shard_scatter(v):
        if shards == 2:
            keep = lax.dynamic_index_in_dim(v, x, 0, keepdims=False)
            give = lax.dynamic_index_in_dim(v, 1 - x, 0, keepdims=False)
            return keep.astype(F32) + lax.ppermute(give, "shard", [(0, 1), (1, 0)]).astype(F32)
        return lax.psum_scatter(v, "shard", scatter_dimension=0, tiled=False).astype(F32)

    def tp_shift(v, bit):
        return lax.ppermute(v, "tp", [(i, i ^ bit) for i in range(tp)])

    token_rows, own_cot, seg = spread(
        tokens, [cotangent, segments.reshape(seqs, length // 128, 128)], length,
        [(ctx, rows, width), (ctx, length // 128, 128)], 0,
    )
    own_tok = lax.dynamic_slice_in_dim(token_rows, q * rows, rows, axis=1).reshape(ctx * rows, width)
    own_cot = own_cot.reshape(ctx * rows, width)
    seg = seg.reshape(full)

    pack = jnp.concatenate([w_out, w_in, w_down], axis=0)
    pair = shard_gather(pack)
    cuts = (0, w_out.shape[0], w_out.shape[0] + w_in.shape[0], pack.shape[0])
    base = jnp.concatenate([pair[:, cuts[i] : cuts[i + 1]].reshape(-1, width) for i in range(3)], axis=0)
    away = tp_shift(base, 2)
    slots = jnp.stack([base, tp_shift(base, 1), away, tp_shift(away, 1)])
    n_out, n_in, n_down = (shards * (cuts[i + 1] - cuts[i]) for i in range(3))
    out_w = slots[:, :n_out].reshape(tp * n_out, width)
    in_w = slots[:, n_out : n_out + n_in]
    down_w = slots[:, n_out + n_in :]
    qkv_w = shard_gather(w_qkv.reshape(-1, 3 * local)).reshape(width, 3 * local)
    affine = shard_gather(jnp.concatenate([norm_gains, norm_shifts], axis=1)).reshape(width, 4)
    affine = affine.astype(F32).T[jnp.array([0, 2, 1, 3])]

    feats = time_features(shard_gather(timesteps).reshape(-1), w_time1.shape[0] * shards).astype(BF)
    n1, n2 = w_time1.shape[0], w_time2.shape[0]
    own_feats = lax.dynamic_slice_in_dim(feats, x * n1, n1, axis=1)
    time_pre = shard_sum(dot(own_feats, w_time1))
    time_hidden = silu_fn(time_pre).astype(BF)
    own_hidden = lax.dynamic_slice_in_dim(time_hidden, x * n2, n2, axis=1)
    time_embed = shard_sum(dot(own_hidden, w_time2))
    te = lax.dynamic_slice_in_dim(time_embed, x * seqs + z, 1, axis=0)

    mixed_low = (token_rows.reshape(full, width).astype(F32) + te).astype(BF)
    joint_t = contract(qkv_w, mixed_low, 0, 1).astype(BF)
    joint_t = jnp.concatenate([joint_t[:local] * jnp.asarray(HEAD_DIM ** -0.5, BF), joint_t[local:]], axis=0)
    aq, ak = mask_rows(seg)
    lo, hi = key_ranges(seg, length, 512)
    att, lse = attend(joint_t, aq, ak, lo, hi, heads, HEAD_DIM, tp, length, 512)
    att_own = swap(att, True, False, 1).reshape(tp * local, ctx * rows)
    out_own, gjs, gatt, g_out, g_in, g_down, sums = middle(
        att_own, own_tok, te, affine, own_cot, out_w, in_w, down_w
    )
    (result,) = spread(out_own.reshape(ctx, rows, width), [], length, [], 2)
    got = swap(gatt.reshape(tp, local, ctx * rows), False, True, 3)
    lo, hi = key_ranges(seg, length, 256)
    dq, dkv = attend_back(joint_t, aq, ak, att, got, lse, lo, hi, heads, HEAD_DIM, tp, length, 256)
    grad_t = jnp.concatenate([dq, dkv], axis=0)
    g_qkv = contract(mixed_low, grad_t, 0, 1).astype(BF)
    terms = contract(grad_t, qkv_w, 0, 1).astype(BF).reshape(ctx, length, width)
    grad_own = gjs.reshape(ctx, rows, width) + fold(terms, 4)
    (grad_tokens,) = spread(grad_own.astype(BF), [], length, [], 5)

    total = jnp.zeros((seqs * shards, width), F32)
    total = lax.dynamic_update_slice_in_dim(total, jnp.sum(grad_own, axis=(0, 1))[None], x * seqs + z, 0)
    total = lax.psum(jnp.concatenate([total, sums[:4]], axis=0), ("shard", "ctx", "tp"))
    grad_embed = total[: seqs * shards].astype(BF)
    own_pre = lax.dynamic_slice_in_dim(time_pre, x * n2, n2, axis=1)
    grad_pre = jax.vjp(silu_fn, own_pre)[1](contract(grad_embed, w_time2, 1, 1))[0].astype(BF)
    grad_pre = jnp.swapaxes(shard_gather(grad_pre), 0, 1).reshape(seqs * shards, width)
    g_time1 = contract(own_feats, grad_pre, 0, 0)
    g_time2 = contract(own_hidden, grad_embed, 0, 0)
    share = width // shards
    affine_sums = lax.dynamic_slice_in_dim(total[seqs * shards :], x * share, share, axis=1)
    g_gains = jnp.stack([affine_sums[0], affine_sums[2]], axis=1)
    g_shifts = jnp.stack([affine_sums[1], affine_sums[3]], axis=1)

    grads = jnp.concatenate([g_out.reshape(tp, n_out, width), g_in, g_down], axis=1)
    near = tp_shift(jnp.stack([grads[1], grads[3]]), 1)
    half0 = (grads[0].astype(F32) + near[0].astype(F32))
    half2 = (grads[2].astype(F32) + near[1].astype(F32)).astype(BF)
    whole = (half0 + tp_shift(half2, 2).astype(F32)).astype(BF)
    marks = (0, n_out, n_out + n_in, n_out + n_in + n_down)
    whole = jnp.concatenate([whole[marks[i] : marks[i + 1]].reshape(shards, -1, width) for i in range(3)], axis=1)
    piece = shard_scatter(whole).astype(BF)
    qkv_piece = shard_scatter(g_qkv.reshape(shards, width // shards, 3 * local)).astype(BF)
    piece = lax.psum(piece, "ctx").astype(F32)
    qkv_piece = lax.psum(qkv_piece, "ctx").astype(F32)
    return (
        result, grad_tokens.astype(F32), g_time1, g_time2, qkv_piece.reshape(w_qkv.shape),
        piece[: cuts[1]], piece[cuts[1] : cuts[2]], piece[cuts[2] :], g_gains, g_shifts,
    )


def solution(mesh):
    placed = (
        P("shard", "ctx", None), P("shard", "ctx"), P("shard"), P("shard", None), P("shard", None),
        P("shard", None, "tp"), P(("tp", "shard"), None), P("shard", "tp"), P(("tp", "shard"), None),
        P("shard", None), P("shard", None), P("shard", "ctx", None),
    )
    return jax.shard_map(
        body,
        mesh=mesh,
        in_specs=placed,
        out_specs=(
            P("shard", "ctx", None), P("shard", "ctx", None), P("shard", None), P("shard", None),
            P("shard", None, "tp"), P(("tp", "shard"), None), P("shard", "tp"), P(("tp", "shard"), None),
            P("shard", None), P("shard", None),
        ),
        check_vma=False,
    )
```

time: 1270 us -> 569 us (0.45)
  waiting for transfers between devices: 688 us -> 67.9 us
  Pallas kernels: 0 us -> 313 us
  matrix products: 205 us -> 14.2 us
  blocking collectives: 147 us -> 39.9 us
  other arithmetic: 131 us -> 54.2 us
  local copies, waits for them, and re-layouts: 77.3 us -> 29.4 us
  starting transfers between devices: 2.84 us -> 32.5 us
    psum x9 -> x1, waiting for transfers between devices: 378 us -> 0.01 us  [body(): qkv_piece = lax.psum(qkv_piece, 'ctx').astype(F32)]
    pallas_call x0 -> x9, Pallas kernels: none -> 313 us  [the longest x3 135 us: spread(): pl.pallas_call(functools.partial(spread_kernel, len(extras)), out_shape=s...]
    dot_general x44 -> x8, matrix products: 205 us -> 14.2 us  [contract(): lax.dot_general(left, right, (((ldim,), (rdim,)), ((), ())), preferred_el...]
    all_gather x10 -> x0, waiting for transfers between devices: 141 us -> none  [the longest x2 41.7 us: step(): lax.all_gather(local_weights[4], 'shard', axis=0, tiled=True)]
    reduce_scatter x9 -> x0, waiting for transfers between devices: 132 us -> none  [the longest x2 31.4 us: step(): lax.psum_scatter(key_terms.astype(jnp.bfloat16), 'ctx', scatter_dimension...]
    all_gather x12 -> x0, blocking collectives: 111 us -> none  [the longest x2 44.9 us: step(): lax.all_gather(local_weights[2], 'shard', axis=0, tiled=True)]
    ppermute x0 -> x14, waiting for transfers between devices: none -> 67.9 us  [the longest x5 29.1 us: shard_gather(): other = lax.ppermute(v, 'shard', [(0, 1), (1, 0)])]
    reduce_sum x18 -> x2, other arithmetic: 57.2 us -> 3.43 us  [the longest x1 2.51 us: body(): jnp.sum(grad_own, axis=(0, 1))[None]]
  transfers between devices with their start and end apart: 31 -> 15, of which waited for: 29 -> 5; matrix products, arithmetic and copies ran while one was open for 18% -> 10% of each run, Pallas kernels for 0% -> 50%
where the time goes in v1:
time: 569 us; the launch traced here: 566 us
  Pallas kernels  313 us (55%)
  waiting for transfers between devices  67.9 us (12%)
  other arithmetic  54.2 us (10%)
  blocking collectives  39.9 us (7%)
  starting transfers between devices  32.5 us (6%)
  local copies, waits for them, and re-layouts  29.4 us (5%)
  between operations  14.5 us (3%)
  matrix products  14.2 us (2%)
    pallas_call x3, Pallas kernels, spread(): pl.pallas_call(functools.partial(spread_kernel, len(extras)), out_shape=s...  135 us
    pallas_call x2, Pallas kernels, swap(): pl.pallas_call(functools.partial(swap_kernel, src_abs, dst_abs), out_shap...  77.2 us
    psum x1, blocking collectives, body(): lax.psum(jnp.concatenate([total, sums[:4]], axis=0), ('shard', 'ctx', 'tp'))  39.9 us
    pallas_call x1, Pallas kernels, middle(): pl.pallas_call(functools.partial(middle_kernel, chunk), out_shape=(shape(...  29.6 us
    ppermute x5, waiting for transfers between devices, shard_gather(): other = lax.ppermute(v, 'shard', [(0, 1), (1, 0)])  29.1 us
    pallas_call x1, Pallas kernels, attend_back(): pl.pallas_call(functools.partial(attend_back_kernel, heads, bk, hd ** (-0...  28 us
    ppermute x2, waiting for transfers between devices, shard_scatter(): lax.ppermute(give, 'shard', [(0, 1), (1, 0)]).astype(F32)  26.4 us
    pallas_call x1, Pallas kernels, fold(): pl.pallas_call(fold_kernel, out_shape=jax.ShapeDtypeStruct((count, rows,...  24.7 us
  transfers between devices with their start and end apart: 15, of which 5 were waited for; matrix products, arithmetic and copies ran while one was open for 10% of the time, Pallas kernels for 50%

profile of v1, /device:TPU:0, one launch (start us, length us, event | category | flops | bytes accessed | tf_op | source)
XLA Modules:
  0.0 566.1 jit_solution(2901049959930317887)
XLA Ops:
  7.2 1.0 constant_dynamic-update-slice_fusion.2
  8.2 1.1 constant_dynamic-update-slice_fusion.1
  9.3 1.1 constant_dynamic-update-slice_fusion
  10.4 3.0 collective-permute-start.5
  13.5 29.1 %collective-permute-done.5 = bf16[864,768]{1,0:T(8,128)(2,1)S(1)} collective-permute-done((bf16[864,768]{1,0:T(8,128)(2,1)S(1)}, bf16[864,768]{1,0:T(8,128)(2,1)S(1)}, u32[]{:S(2)}, u32[]{:S(2)}) %collective-permute-start.5) | collective-permute-done | bytes 1327136 | tf_op jit(solution)/shard_map/ppermute | solution.py:545
  43.3 1.8 fusion.20
  45.1 1.8 collective-permute-start.7
  46.9 1.5 collective-permute-start.1
  48.9 1.6 collective-permute-start.4
  51.1 69.0 %spread.3 = (bf16[4,512,768]{2,1,0:T(8,128)(2,1)}, bf16[4,128,768]{2,1,0:T(8,128)(2,1)}, s32[4,4,128]{2,1,0:T(4,128)}) custom-call(bf16[4,512,768]{2,1,0:T(8,128)(2,1)} %src.1, bf16[4,512,768]{2,1,0:T(8,128)(2,1)} %refs_0_.1, s32[4,4,128]{2,1,0:T(4,128)} %reshape.150.refs_1_), custom_call_target="tpu_custom_call" | custom-call | tf_op jit(solution)/shard_map/spread/pallas_call | solution.py:340
  120.1 0.8 slice.90
  120.9 0.8 slice.91
  122.6 0.7 concatenate.32.aq_ref
  123.3 0.9 convert_reduce_fusion
  124.3 2.1 constant_dynamic-slice_fusion.3
  127.6 0.8 maximum_maximum_fusion.ak_ref
  129.4 1.5 collective-permute-start.2
  130.9 2.3 collective-permute-done.2
  133.4 1.5 collective-permute-start.3
  134.9 1.2 gather_fusion
  136.1 1.2 collective-permute-done.3
  137.9 2.5 add_convert_fusion
  140.4 1.6 fusion.4
  142.0 2.0 convolution_convert_fusion.1
  144.1 1.3 slice.122.kv_ref
  145.4 0.9 slice_multiply_fusion.qt_ref
  146.4 19.0 %attend.1 = (bf16[4,192,512]{2,1,0:T(8,128)(2,1)}, f32[3,1,2048]{2,1,0:T(1,128)}) custom-call(s32[4]{0:T(128)} %get-tuple-element.72.lo_ref, s32[4]{0:T(128)} %get-tuple-element.69.hi_ref, bf16[192,2048]{1,0:T(8,128)(2,1)} %slice_multiply_fusion.qt_ref, bf16[384,2048]{1,0:T(8,128)(2,1)} %slice.122.kv_ref, bf16[64,2048]{1,0:T(8,128)(2,1)} %concatenate.32.aq_ref, ...), custom_call_target="tpu_custom_call" | custom-call | flops 3221225472 | bytes 3145728 | tf_op jit(solution)/shard_map/attend/pallas_call | solution.py:100
  165.4 13.6 %swap.2 = bf16[4,192,512]{2,1,0:T(8,128)(2,1)} custom-call(bf16[4,192,512]{2,1,0:T(8,128)(2,1)} %get-tuple-element.26.src.ot_ref), custom_call_target="tpu_custom_call" | custom-call | tf_op jit(solution)/shard_map/swap/pallas_call | solution.py:372
  179.0 8.0 %pad_maximum_fusion.2 = (bf16[4,768,768]{2,1,0:T(8,128)(2,1)}, bf16[4,768,768]{2,1,0:T(8,128)(2,1)}) fusion(bf16[1,1728,768]{2,1,0:T(8,128)(2,1)} %bitcast.22, bf16[1,1728,768]{2,1,0:T(8,128)(2,1)} %bitcast.21, bf16[1,1728,768]{2,1,0:T(8,128)(2,1)} %bitcast.20, bf16[1,1728,768]{2,1,0:T(8,128)(2,1)S(1)} %get-tuple-element.50), kind=kLoop, calls=%fused_computation.9 | loop fusion | flops 37748736 | bytes 20054016 | tf_op jit(solution)/shard_map/stack | solution.py:577
  187.0 2.2 pad_maximum_fusion.8
  189.2 29.6 %middle.1 = (bf16[512,768]{1,0:T(8,128)(2,1)}, f32[512,768]{1,0:T(8,128)}, bf16[768,512]{1,0:T(8,128)(2,1)}, bf16[768,768]{1,0:T(8,128)(2,1)}, bf16[4,768,768]{2...) custom-call(bf16[768,512]{1,0:T(8,128)(2,1)} %bitcast.107, bf16[512,768]{1,0:T(8,128)(2,1)} %bitcast.105, ...), custom_call_target="tpu_custom_call" | custom-call | flops 16307453952 | bytes 56623104 | tf_op jit(solution)/shard_map/middle/pallas_call | solution.py:511
  218.9 5.5 pad_maximum_fusion
  225.3 8.7 %collective-permute-done.11 = bf16[2,1728,768]{2,1,0:T(8,128)(2,1)S(1)} collective-permute-done((bf16[2,1728,768]{2,1,0:T(8,128)(2,1)S(1)}, bf16[2,1728,768]{2,1,0:T(8,128)(2,1)S(1)}, u32[]{:S(2)}, u32[]{:S(2)}) %collective-permute-start.11) | collective-permute-done | bytes 5308448 | tf_op jit(solution)/shard_map/ppermute | solution.py:562
  234.0 2.8 fusion.2
  237.2 1.5 collective-permute-start.12
  238.7 4.2 fusion
  242.8 63.6 %swap.3.gt_ref = bf16[4,192,512]{2,1,0:T(8,128)(2,1)} custom-call(bf16[4,192,512]{2,1,0:T(8,128)(2,1)} %bitcast.106), custom_call_target="tpu_custom_call" | custom-call | tf_op jit(solution)/shard_map/swap/pallas_call | solution.py:372
  306.4 28.0 %attend_back.1 = (bf16[192,2048]{1,0:T(8,128)(2,1)}, bf16[384,2048]{1,0:T(8,128)(2,1)}) custom-call(s32[4]{0:T(128)} %get-tuple-element.73.lo_ref, s32[4]{0:T(128)} %get-tuple-element.68.hi_ref, bf16[192,2048]{1,0:T(8,128)(2,1)} %slice_multiply_fusion.qt_ref, bf16[384,2048]{1,0:T(8,128)(2,1)} %slice.122.kv_ref, bf16[64,2048]{1,0:T(8,128)(2,1)} %concatenate.32.aq_ref, ...), custom_call_target="tpu_custom_call" | custom-call | flops 8053063680 | bytes 6291456 | tf_op jit(solution)/shard_map/attend_back/pallas_call | solution.py:210
  334.4 1.3 constant_dynamic-update-slice_fusion.4
  336.2 4.3 fusion.1
  340.9 1.2 dynamic-slice_bitcast_fusion
  342.1 15.8 %collective-permute-start.13 = (bf16[864,768]{1,0:T(8,128)(2,1)}, bf16[864,768]{1,0:T(8,128)(2,1)}, u32[]{:S(2)}, u32[]{:S(2)}) collective-permute-start(bf16[864,768]{1,0:T(8,128)(2,1)} %dynamic-slice_bitcast_fusion), channel_id=1, source_target_pairs={{0,16},{16,0},{1,17},{17,1},{2,18},{18,2},{3,19},{19,3},{4,20},{20... | collective-permute-start | bytes 3981320 | tf_op jit(solution)/shard_map/ppermute | solution.py:558
  357.9 2.9 convolution_convert_fusion.2
  360.8 2.9 reshape.164
  363.7 4.3 constant_dynamic-slice_fusion.2
  368.0 0.8 copy.37
  368.8 1.0 collective-permute-start.10
  369.9 26.4 %collective-permute-done.10 = bf16[384,576]{0,1:T(8,128)(2,1)} collective-permute-done((bf16[384,576]{0,1:T(8,128)(2,1)}, bf16[384,576]{0,1:T(8,128)(2,1)}, u32[]{:S(2)}, u32[]{:S(2)}) %collective-permute-start.10) | collective-permute-done | bytes 442400 | tf_op jit(solution)/shard_map/ppermute | solution.py:558
  396.3 2.2 fusion.5
  398.4 2.7 fusion.3
  401.2 6.2 %convolution_convert_fusion = bf16[2048,768]{1,0:T(8,128)(2,1)} fusion(bf16[576,2048]{1,0:T(8,128)(2,1)} %copy-done.9, bf16[768,576]{0,1:T(8,128)(2,1)} %bitcast.104), kind=kOutput, calls=%fused_computation.13 | convolution fusion | flops 1813512192 | bytes 6389760 | tf_op jit(solution)/shard_map/dot_general | solution.py:37
  407.4 24.7 %fold.1 = f32[4,128,768]{2,1,0:T(8,128)} custom-call(bf16[4,512,768]{2,1,0:T(8,128)(2,1)} %bitcast.94), custom_call_target="tpu_custom_call" | custom-call | tf_op jit(solution)/shard_map/fold/pallas_call | solution.py:420
  432.1 2.5 add_reduce_fusion
  434.7 39.9 %psum.21 = f32[12,768]{1,0:T(8,128)S(1)} all-reduce(f32[12,768]{1,0:T(8,128)S(1)} %pad_maximum_fusion.9), channel_id=1, replica_groups=mesh['shard'=2,'ctx'=4,'tp'=4] {'shard','ctx','tp'}, use_global_device_ids=true, to_apply=%region_3.4 | all-reduce | flops 9216 | bytes 73728 | tf_op jit(solution)/shard_map/psum | solution.py:617
  474.9 2.3 collective-permute-start.9
  477.8 1.4 fusion.9
  479.8 32.3 %spread.5 = bf16[4,512,768]{2,1,0:T(8,128)(2,1)} custom-call(bf16[4,128,768]{2,1,0:T(8,128)(2,1)} %get-tuple-element.55.src), custom_call_target="tpu_custom_call" | custom-call | tf_op jit(solution)/shard_map/spread/pallas_call | solution.py:340
  512.1 5.1 convert_element_type.138
  517.2 33.7 %spread.4 = bf16[4,512,768]{2,1,0:T(8,128)(2,1)} custom-call(bf16[4,128,768]{2,1,0:T(8,128)(2,1)} %bitcast.108), custom_call_target="tpu_custom_call" | custom-call | tf_op jit(solution)/shard_map/spread/pallas_call | solution.py:340
  551.0 1.0 fusion.12
  552.0 3.0 fusion.25
  554.9 1.6 slice.136
  556.6 1.0 reshape.166
  557.5 1.7 copy.45
  (92 shorter events, 9.6 us)
Async XLA Ops:
  7.2 126.1 %copy-start = (bf16[384,768]{1,0:T(8,128)(2,1)S(1)}, bf16[384,768]{1,0:T(8,128)(2,1)}, u32[]{:S(2)}) copy-start(bf16[384,768]{1,0:T(8,128)(2,1)} %param.17) | copy-start | bytes 1769476
  7.2 544.8 %all-reduce.4.cloned.1.call-start = ((), (), s32[]{:S(2)}) async-start(), calls=%async_computation | async-start | bytes 3538944 | tf_op jit(solution)/shard_map/psum | solution.py:639
  10.4 32.2 %collective-permute-start.5 = (bf16[864,768]{1,0:T(8,128)(2,1)S(1)}, bf16[864,768]{1,0:T(8,128)(2,1)S(1)}, u32[]{:S(2)}, u32[]{:S(2)}) collective-permute-start(bf16[864,768]{1,0:T(8,128)(2,1)S(1)} %constant_dynamic-update-slice_fusion), channel_id=1, source_target_pairs={{0,16},{16,0},{1,17},{17,1},{2,18},{18,2},{3,19},{19,3},{4,20},{20... | collective-permute-start | bytes 3981320 | tf_op jit(solution)/shard_map/ppermute | solution.py:545
  43.2 3.7 copy-start.15
  43.2 5.7 %copy-start.13 = (bf16[384,2]{0,1:T(2,128)(2,1)S(1)}, bf16[384,2]{0,1:T(2,128)(2,1)}, u32[]{:S(2)}) copy-start(bf16[384,2]{0,1:T(2,128)(2,1)} %param.23) | copy-start | bytes 4612
  43.3 5.7 %copy-start.14 = (bf16[384,2]{0,1:T(2,128)(2,1)S(1)}, bf16[384,2]{0,1:T(2,128)(2,1)}, u32[]{:S(2)}) copy-start(bf16[384,2]{0,1:T(2,128)(2,1)} %param.22) | copy-start | bytes 4612
  43.3 7.2 %copy-start.11 = (s32[4,512]{1,0:T(4,128)S(1)}, s32[4,512]{1,0:T(4,128)}, u32[]{:S(2)}) copy-start(s32[4,512]{1,0:T(4,128)} %param.14) | copy-start | bytes 24580
  45.1 84.0 %collective-permute-start.7 = (bf16[1728,768]{1,0:T(8,128)(2,1)}, bf16[1728,768]{1,0:T(8,128)(2,1)}, u32[]{:S(2)}, u32[]{:S(2)}) collective-permute-start(bf16[1728,768]{1,0:T(8,128)(2,1)} %get-tuple-element.51), channel_id=1, source_target_pairs={{0,2},{1,3},{2,0},{3,1},{4,6},{5,7},{6,4},{7,5},{8,10},{9,11},{10,... | collective-permute-start | bytes 7962632 | tf_op jit(solution)/shard_map/ppermute | solution.py:562
  46.9 81.5 %collective-permute-start.1 = (s32[4]{0:T(128)S(1)}, s32[4]{0:T(128)S(1)}, u32[]{:S(2)}, u32[]{:S(2)}) collective-permute-start(s32[4]{0:T(128)S(1)} %copy-done.15), channel_id=1, source_target_pairs={{0,16},{16,0},{1,17},{17,1},{2,18},{18,2},{3,19},{19,3},{4,20},{20... | collective-permute-start | bytes 56 | tf_op jit(solution)/shard_map/ppermute | solution.py:545
  48.4 92.0 %collective-permute-start = (bf16[384,576]{0,1:T(8,128)(2,1)}, bf16[384,576]{0,1:T(8,128)(2,1)}, u32[]{:S(2)}, u32[]{:S(2)}) collective-permute-start(bf16[384,576]{0,1:T(8,128)(2,1)} %bitcast.2), channel_id=1, source_target_pairs={{0,16},{16,0},{1,17},{17,1},{2,18},{18,2},{3,19},{19,3},{4,20},{20... | collective-permute-start | bytes 1327112 | tf_op jit(solution)/shard_map/ppermute | solution.py:545
  48.9 82.0 %collective-permute-start.4 = (bf16[384,4]{0,1:T(4,128)(2,1)S(1)}, bf16[384,4]{0,1:T(4,128)(2,1)S(1)}, u32[]{:S(2)}, u32[]{:S(2)}) collective-permute-start(bf16[384,4]{0,1:T(4,128)(2,1)S(1)} %get-tuple-element.65), channel_id=1, source_target_pairs={{0,16},{16,0},{1,17},{17,1},{2,18},{18,2},{3,19},{19,3},{4,20},{20... | collective-permute-start | bytes 9224 | tf_op jit(solution)/shard_map/ppermute | solution.py:545
  51.1 72.2 %copy-start.16 = (s32[4]{0:T(128)S(1)}, s32[4]{0:T(128)}, u32[]{:S(2)}) copy-start(s32[4]{0:T(128)} %constant.121) | copy-start | bytes 52
  51.1 78.1 %copy-start.10 = (bf16[64,768]{1,0:T(8,128)(2,1)S(1)}, bf16[64,768]{1,0:T(8,128)(2,1)}, u32[]{:S(2)}) copy-start(bf16[64,768]{1,0:T(8,128)(2,1)} %param.16) | copy-start | bytes 294916
  128.7 50.2 %collective-permute-start.6 = (bf16[1728,768]{1,0:T(8,128)(2,1)}, bf16[1728,768]{1,0:T(8,128)(2,1)}, u32[]{:S(2)}, u32[]{:S(2)}) collective-permute-start(bf16[1728,768]{1,0:T(8,128)(2,1)} %get-tuple-element.51), channel_id=1, source_target_pairs={{0,1},{1,0},{2,3},{3,2},{4,5},{5,4},{6,7},{7,6},{8,9},{9,8},{10,11... | collective-permute-start | bytes 7962632 | tf_op jit(solution)/shard_map/ppermute | solution.py:562
  129.1 49.9 %collective-permute-start.8 = (bf16[1728,768]{1,0:T(8,128)(2,1)}, bf16[1728,768]{1,0:T(8,128)(2,1)}, u32[]{:S(2)}, u32[]{:S(2)}) collective-permute-start(bf16[1728,768]{1,0:T(8,128)(2,1)} %collective-permute-done.7), channel_id=1, source_target_pairs={{0,1},{1,0},{2,3},{3,2},{4,5},{5,4},{6,7},{7,6},{8,9},{9,8},{10,11... | collective-permute-start | bytes 7962632 | tf_op jit(solution)/shard_map/ppermute | solution.py:562
  129.4 3.8 collective-permute-start.2
  133.4 3.8 collective-permute-start.3
  142.0 2.0 copy-start.7
  224.3 9.7 %copy-start.1 = (bf16[4,1728,768]{2,1,0:T(8,128)(2,1)}, bf16[4,1728,768]{2,1,0:T(8,128)(2,1)S(1)}, u32[]{:S(2)}) copy-start(bf16[4,1728,768]{2,1,0:T(8,128)(2,1)S(1)} %pad_maximum_fusion) | copy-start | bytes 31850500
  225.2 8.8 %collective-permute-start.11 = (bf16[2,1728,768]{2,1,0:T(8,128)(2,1)S(1)}, bf16[2,1728,768]{2,1,0:T(8,128)(2,1)S(1)}, u32[]{:S(2)}, u32[]{:S(2)}) collective-permute-start(bf16[2,1728,768]{2,1,0:T(8,128)(2,1)S(1)} %pad_maximum_fusion.1), channel_id=1, source_target_pairs={{0,1},{1,0},{2,3},{3,2},{4,5},{5,4},{6,7},{7,6},{8,9},{9,8},{10,11... | collective-permute-start | bytes 15925256 | tf_op jit(solution)/shard_map/ppermute | solution.py:562
  234.0 3.2 copy-start.3
  237.2 99.0 %collective-permute-start.12 = (bf16[1728,768]{1,0:T(8,128)(2,1)}, bf16[1728,768]{1,0:T(8,128)(2,1)S(1)}, u32[]{:S(2)}, u32[]{:S(2)}) collective-permute-start(bf16[1728,768]{1,0:T(8,128)(2,1)} %fusion.2), channel_id=1, source_target_pairs={{0,2},{1,3},{2,0},{3,1},{4,6},{5,7},{6,4},{7,5},{8,10},{9,11},{10,... | collective-permute-start | bytes 7962632 | tf_op jit(solution)/shard_map/ppermute | solution.py:562
  334.4 1.6 copy-start.6
  336.2 21.7 %copy-start.9 = (bf16[576,2048]{1,0:T(8,128)(2,1)}, bf16[576,2048]{1,0:T(8,128)(2,1)S(1)}, u32[]{:S(2)}) copy-start(bf16[576,2048]{1,0:T(8,128)(2,1)S(1)} %constant_dynamic-update-slice_fusion.3) | copy-start | bytes 7077892
  340.7 17.2 %copy-start.4 = (bf16[2048,768]{1,0:T(8,128)(2,1)S(1)}, bf16[2048,768]{1,0:T(8,128)(2,1)}, u32[]{:S(2)}) copy-start(bf16[2048,768]{1,0:T(8,128)(2,1)} %fusion) | copy-start | bytes 9437188
  342.1 56.3 %collective-permute-start.13 = (bf16[864,768]{1,0:T(8,128)(2,1)}, bf16[864,768]{1,0:T(8,128)(2,1)}, u32[]{:S(2)}, u32[]{:S(2)}) collective-permute-start(bf16[864,768]{1,0:T(8,128)(2,1)} %dynamic-slice_bitcast_fusion), channel_id=1, source_target_pairs={{0,16},{16,0},{1,17},{17,1},{2,18},{18,2},{3,19},{19,3},{4,20},{20... | collective-permute-start | bytes 3981320 | tf_op jit(solution)/shard_map/ppermute | solution.py:558
  368.8 27.4 %collective-permute-start.10 = (bf16[384,576]{0,1:T(8,128)(2,1)}, bf16[384,576]{0,1:T(8,128)(2,1)}, u32[]{:S(2)}, u32[]{:S(2)}) collective-permute-start(bf16[384,576]{0,1:T(8,128)(2,1)} %bitcast.89), channel_id=1, source_target_pairs={{0,16},{16,0},{1,17},{17,1},{2,18},{18,2},{3,19},{19,3},{4,20},{20... | collective-permute-start | bytes 1327112 | tf_op jit(solution)/shard_map/ppermute | solution.py:558
  407.4 24.7 %copy-start.5 = (f32[512,768]{1,0:T(8,128)S(1)}, f32[512,768]{1,0:T(8,128)}, u32[]{:S(2)}) copy-start(f32[512,768]{1,0:T(8,128)} %get-tuple-element.29) | copy-start | bytes 4718596
  432.1 2.5 copy-start.12
  474.9 76.1 %collective-permute-start.9 = (bf16[8,384]{1,0:T(8,128)(2,1)S(1)}, bf16[8,384]{1,0:T(8,128)(2,1)S(1)}, u32[]{:S(2)}, u32[]{:S(2)}) collective-permute-start(bf16[8,384]{1,0:T(8,128)(2,1)S(1)} %add_convert_fusion.3), channel_id=1, source_target_pairs={{0,16},{16,0},{1,17},{17,1},{2,18},{18,2},{3,19},{19,3},{4,20},{20... | collective-permute-start | bytes 18440 | tf_op jit(solution)/shard_map/ppermute | solution.py:545
  551.9 4.6 copy-start.8
  552.0 5.6 copy-start.2
Sparse Core Ops, SparseCore 0:
  401.3 74.9 all-reduce.3

commit v2 on v1

--- a/solution.py
+++ b/solution.py
@@ -349,6 +349,178 @@
     )(src, *extras)
 
 
+def front_kernel(
+    src, cot, seg, w_out, w_in, w_down, w_qkv, affine, feats, w_time1, w_time2,
+    dst, own_cot, own_seg, out_w, in_w, down_w, qkv_w, affine_all, te, pre, hidden,
+    feat, part1, part2, embed, hold_tok, hold_cot, hold_qkv, hold_out, hold_in, hold_down, loc, zs, zr, ss, rs,
+):
+    x, z, q = lax.axis_index("shard"), lax.axis_index("ctx"), lax.axis_index("tp")
+    count = lax.axis_size("ctx")
+    seqs = src.shape[0]
+    rows = dst.shape[1] // lax.axis_size("tp")
+    other, mate, far = 1 - x, q ^ 1, q ^ 2
+    mine = pl.ds(pl.multiple_of(q * rows, rows), rows)
+    far_rows = pl.ds(pl.multiple_of(far * rows, rows), rows)
+    ids = iter(range(ss.shape[0]))
+    every = []
+
+    def remote(a, b, **where):
+        i = next(ids)
+        copy = send(a, b, ss.at[i], rs.at[i], **where)
+        copy.start()
+        every.append(copy)
+        return copy
+
+    to = ctx_peers(z, count)
+
+    def hop(a, b, base, peer):
+        return pltpu.make_async_remote_copy(
+            src_ref=a, dst_ref=b, send_sem=zs.at[base, peer], recv_sem=zr.at[base, z],
+            device_id={"ctx": peer}, device_id_type=MESH,
+        )
+
+    def landed(a, b, base, peer):
+        return pltpu.make_async_remote_copy(
+            src_ref=a, dst_ref=b, send_sem=zs.at[base, peer], recv_sem=zr.at[base, peer],
+            device_id={"ctx": peer}, device_id_type=MESH,
+        )
+
+    pairs = [(src.at[z], hold_tok, dst.at[z]), (cot.at[z, mine], hold_cot, own_cot.at[z]),
+             (w_qkv, hold_qkv, qkv_w.at[x]), (w_out, hold_out, out_w.at[0, x]),
+             (w_in, hold_in, in_w.at[0, x]), (w_down, hold_down, down_w.at[0, x])]
+    loads = [pltpu.make_async_copy(a, h, loc.at[0, i]) for i, (a, h, _) in enumerate(pairs)]
+    keep = [pltpu.make_async_copy(h, b, loc.at[1, i]) for i, (_, h, b) in enumerate(pairs)]
+    for copy in loads:
+        copy.start()
+    meet([{"ctx": p} for p in to] + [{"tp": mate}, {"tp": far}, {"shard": other}])
+    feat[pl.ds(x, 1)] = feats[...][None]
+    feat_in = remote(feats, feat.at[x], shard=other)
+    for p in to:
+        hop(seg.at[p], own_seg.at[z], 0, p).start()
+    for p in to:
+        hop(src.at[p, mine], dst.at[z, mine], 1, p).start()
+    y_in = remote(w_in, in_w.at[2, x], tp=far)
+    y_down = remote(w_down, down_w.at[2, x], tp=far)
+    y_out = remote(w_out, out_w.at[2, x], tp=far)
+    for p in to:
+        hop(cot.at[p, mine], own_cot.at[z], 2, p).start()
+    for piece, whole in ((w_out, out_w), (w_in, in_w), (w_down, down_w)):
+        remote(piece, whole.at[1, x], tp=mate)
+    own_seg[pl.ds(z, 1)] = seg[pl.ds(z, 1)]
+    affine_all[pl.ds(x, 1)] = affine[...][None]
+    for load, copy in zip(loads, keep):
+        load.wait()
+        copy.start()
+
+    xf = x.astype(F32)
+    feat_in.wait_recv()
+    all_feats = jnp.concatenate([feat[0, :seqs], feat[1, :seqs]], axis=0)
+    half = feats.shape[1] // 2
+    own = (all_feats[:, :half] * (1.0 - xf) + all_feats[:, half:] * xf).astype(BF)
+    part1[0] = dot(own, w_time1[...])
+    part1_in = remote(part1.at[0], part1.at[1], shard=other)
+    remote(w_qkv, qkv_w.at[x], shard=other)
+    remote(affine, affine_all.at[x], shard=other)
+    part1_in.wait_recv()
+    pre[...] = part1[0] + part1[1]
+    hid = silu_fn(pre[...])
+    half = hid.shape[1] // 2
+    own = (hid[:, :half] * (1.0 - xf) + hid[:, half:] * xf).astype(BF)
+    hidden[...] = own
+    part2[0] = dot(own, w_time2[...])
+    part2_in = remote(part2.at[0], part2.at[1], shard=other)
+    x_down = remote(w_down, down_w.at[0, x], shard=other)
+    x_in = remote(w_in, in_w.at[0, x], shard=other)
+    x_out = remote(w_out, out_w.at[0, x], shard=other)
+
+    def pass_core(whole, slot, shard):
+        remote(whole.at[slot, shard], whole.at[slot + 1, shard], tp=mate)
+
+    across = []
+
+    def pass_tokens(k):
+        landed(src.at[to[k], mine], dst.at[to[k], mine], 1, to[k]).wait_recv()
+        at = dst.at[to[k], mine]
+        across.append(remote(at, at, tp=far))
+        remote(at, at, tp=mate)
+
+    pass_tokens(0)
+    pass_tokens(1)
+    y_in.wait_recv()
+    diag_in = remote(in_w.at[2, x], in_w.at[2, x], shard=other)
+    pass_core(in_w, 2, x)
+    pass_tokens(2)
+    x_down.wait_recv()
+    diag_down = remote(down_w.at[0, other], down_w.at[2, other], tp=far)
+    pass_core(down_w, 0, other)
+    part2_in.wait_recv()
+    embed[...] = part2[0] + part2[1]
+    te[...] = embed[pl.ds(x * seqs + z, 1), :]
+    y_down.wait_recv()
+    pass_core(down_w, 2, x)
+    y_out.wait_recv()
+    diag_out = remote(out_w.at[2, x], out_w.at[2, x], shard=other)
+    pass_core(out_w, 2, x)
+    x_in.wait_recv()
+    pass_core(in_w, 0, other)
+    x_out.wait_recv()
+    pass_core(out_w, 0, other)
+    for k in range(len(to)):
+        across[k].wait_recv()
+        at = dst.at[to[k], far_rows]
+        remote(at, at, tp=mate)
+    diag_in.wait_recv()
+    pass_core(in_w, 2, other)
+    diag_down.wait_recv()
+    pass_core(down_w, 2, other)
+    diag_out.wait_recv()
+    pass_core(out_w, 2, other)
+    early = [feat_in, part1_in, part2_in, x_in, y_down, y_out, y_in, x_down, x_out, diag_in, diag_down, diag_out]
+    early += across
+    for copy in every:
+        copy.wait_send()
+        if all(copy is not e for e in early):
+            copy.wait_recv()
+    for p in to:
+        hop(seg.at[p], own_seg.at[z], 0, p).wait_send()
+        hop(src.at[p, mine], dst.at[z, mine], 1, p).wait_send()
+        hop(cot.at[p, mine], own_cot.at[z], 2, p).wait_send()
+        landed(seg.at[p], own_seg.at[p], 0, p).wait_recv()
+        landed(cot.at[p, mine], own_cot.at[p], 2, p).wait_recv()
+    for copy in keep:
+        copy.wait()
+
+
+def front(tokens, cot, seg, w_out, w_in, w_down, w_qkv, affine, feats, w_time1, w_time2, ident):
+    seqs, length, width = tokens.shape
+    count, tp = lax.axis_size("ctx"), lax.axis_size("tp")
+    sem = pltpu.SemaphoreType.DMA
+    shape = jax.ShapeDtypeStruct
+    vmem = pl.BlockSpec(memory_space=pltpu.VMEM)
+    hbm = pl.BlockSpec(memory_space=pl.ANY)
+    time_rows = 2 * seqs
+    outs = [
+        shape((count, length, width), BF), shape((count, length // tp, width), BF), shape((count,) + seg.shape[1:], seg.dtype),
+        shape((tp, 2) + w_out.shape, BF), shape((tp, 2) + w_in.shape, BF), shape((tp, 2) + w_down.shape, BF),
+        shape((2,) + w_qkv.shape, BF), shape((2,) + affine.shape, F32),
+        shape((1, width), F32), shape((time_rows, width), F32), shape((time_rows, w_time2.shape[0]), BF),
+    ]
+    return pl.pallas_call(
+        front_kernel,
+        out_shape=outs,
+        in_specs=[hbm, hbm, vmem, hbm, hbm, hbm, hbm, vmem, vmem, vmem, vmem],
+        out_specs=[hbm, hbm, vmem, hbm, hbm, hbm, hbm, vmem, vmem, vmem, vmem],
+        scratch_shapes=[
+            pltpu.VMEM((2,) + feats.shape, F32), pltpu.VMEM((2, time_rows, width), F32), pltpu.VMEM((2, time_rows, width), F32),
+            pltpu.VMEM((time_rows, width), F32), pltpu.VMEM((length, width), BF), pltpu.VMEM((length // tp, width), BF),
+            pltpu.VMEM(w_qkv.shape, BF), pltpu.VMEM(w_out.shape, BF), pltpu.VMEM(w_in.shape, BF), pltpu.VMEM(w_down.shape, BF),
+            sem((2, 8)), sem((3, count)), sem((3, count)), sem((48,)), sem((48,)),
+        ],
+        compiler_params=pltpu.CompilerParams(collective_id=ident, has_side_effects=True),
+        name="front",
+    )(tokens, cot, seg, w_out, w_in, w_down, w_qkv, affine, feats, w_time1, w_time2)
+
+
 def swap_kernel(src_abs, dst_abs, src, dst, ss, rs, loc):
     q = lax.axis_index("tp")
     count = lax.axis_size("tp")
@@ -427,6 +599,343 @@
         compiler_params=pltpu.CompilerParams(collective_id=ident, has_side_effects=True),
         name="fold",
     )(terms)
+
+
+def ctx_peers(z, count):
+    if count != 4:
+        return tuple(lax.rem(z + d, count) for d in range(1, count))
+    upper = z // 2
+    return z ^ 1, 2 - upper, 3 - 3 * upper
+
+
+def add_rows(out, terms, step=96):
+    def body(i, carry):
+        r = pl.ds(pl.multiple_of(i * step, step), step)
+        total = terms[0][r, :].astype(F32)
+        for t in terms[1:]:
+            total = total + t[r, :].astype(F32)
+        out[r, :] = total.astype(out.dtype)
+        return carry
+
+    lax.fori_loop(0, out.shape[0] // step, body, 0)
+
+
+def turn_kernel(
+    gatt, g_out, g_in, g_down, got, send_y, keep_y, send_x, keep_x,
+    hold, own_out, own_in, own_down, near_out, near_in, near_down, loc, ss, rs,
+):
+    x, q = lax.axis_index("shard"), lax.axis_index("tp")
+    ids = iter(range(ss.shape[0]))
+    every = []
+
+    def remote(a, b, **where):
+        i = next(ids)
+        copy = send(a, b, ss.at[i], rs.at[i], **where)
+        copy.start()
+        every.append(copy)
+        return copy
+
+    pairs = [(gatt.at[0], hold)]
+    for i, t in ((0, 0), (1, 2)):
+        pairs += [(g_in.at[t], own_in.at[i]), (g_out.at[t], own_out.at[i]), (g_down.at[t], own_down.at[i])]
+    loads = [pltpu.make_async_copy(a, b, loc.at[i]) for i, (a, b) in enumerate(pairs)]
+    for copy in loads:
+        copy.start()
+    meet([{"tp": q ^ r} for r in (1, 2, 3)])
+    for r in (2, 3, 1):
+        remote(gatt.at[r], got.at[q], tp=q ^ r)
+    come_in = [remote(g_in.at[t], near_in.at[i], tp=q ^ 1) for i, t in ((1, 3), (0, 1))]
+    come_out = [remote(g_out.at[t], near_out.at[i], tp=q ^ 1) for i, t in ((1, 3), (0, 1))]
+    come_down = [remote(g_down.at[t], near_down.at[i], tp=q ^ 1) for i, t in ((1, 3), (0, 1))]
+    for copy in loads:
+        copy.wait()
+    own = pltpu.make_async_copy(hold, got.at[q], loc.at[len(pairs)])
+    own.start()
+    come_in[0].wait_recv()
+    add_rows(send_y, (own_in.at[1], near_in.at[1]))
+    for copy in come_out + come_down:
+        copy.wait_recv()
+    n_out, n_down = own_out.shape[1] // 2, own_down.shape[1] // 2
+    for i in (1, 0):
+        for shard, to in ((1 - x, send_x), (x, keep_x)):
+            r = pl.ds(pl.multiple_of(shard * n_out, n_out), n_out)
+            add_rows(to.at[i, pl.ds(0, n_out)], (own_out.at[i, r], near_out.at[i, r]))
+            r = pl.ds(pl.multiple_of(shard * n_down, n_down), n_down)
+            add_rows(to.at[i, pl.ds(n_out, n_down)], (own_down.at[i, r], near_down.at[i, r]))
+    come_in[1].wait_recv()
+    add_rows(keep_y, (own_in.at[0], near_in.at[0]))
+    for i, copy in enumerate(every):
+        copy.wait_send()
+        if i < 3:
+            copy.wait_recv()
+    own.wait()
+
+
+def turn(gatt, g_out, g_in, g_down, ident):
+    sem = pltpu.SemaphoreType.DMA
+    shape = jax.ShapeDtypeStruct
+    vmem, hbm = pl.BlockSpec(memory_space=pltpu.VMEM), pl.BlockSpec(memory_space=pl.ANY)
+    width = g_in.shape[2]
+    both = shape((2, (g_out.shape[1] + g_down.shape[1]) // 2, width), BF)
+    two = lambda w: pltpu.VMEM((2,) + w.shape[1:], BF)
+    return pl.pallas_call(
+        turn_kernel,
+        out_shape=(shape(gatt.shape, BF), shape(g_in.shape[1:], BF), shape(g_in.shape[1:], BF), both, both),
+        in_specs=[hbm] * 4,
+        out_specs=[hbm, vmem, vmem, vmem, vmem],
+        scratch_shapes=[pltpu.VMEM(gatt.shape[1:], BF)] + [two(w) for w in (g_out, g_in, g_down)] * 2
+        + [sem((8,)), sem((9,)), sem((9,))],
+        compiler_params=pltpu.CompilerParams(collective_id=ident, has_side_effects=True),
+        name="turn",
+    )(gatt, g_out, g_in, g_down)
+
+
+def tail_kernel(
+    chunks, terms, gjs, sums, own_out, in_y, keep_y, in_x, keep_x, g_qkv,
+    result, gtok, o_in, o_both, o_qkv, totals,
+    tq, near, relay, away, low, x_give, x_take, y_give, y_take, qkv_take, m_in, m_both, m_qkv,
+    box_in, box_both, box_qkv, mid_in, mid_both, mid_qkv, f_in, f_both, f_qkv,
+    small, small_tp, small_z, small_x, loc, zs, zr, cs, cr, ss, rs,
+):
+    x, z, q = lax.axis_index("shard"), lax.axis_index("ctx"), lax.axis_index("tp")
+    count, rows, width = own_out.shape
+    other, mate, far = 1 - x, q ^ 1, q ^ 2
+    mine = pl.ds(pl.multiple_of(q * rows, rows), rows)
+    far_rows = pl.ds(pl.multiple_of(far * rows, rows), rows)
+    ids = iter(range(ss.shape[0]))
+    every, early = [], []
+
+    def quarter(p):
+        return pl.ds(pl.multiple_of(p * rows, rows), rows)
+
+    def remote(a, b, **where):
+        i = next(ids)
+        copy = send(a, b, ss.at[i], rs.at[i], **where)
+        copy.start()
+        every.append(copy)
+        return copy
+
+    def arrive(copy):
+        copy.wait_recv()
+        early.append(copy)
+
+    to = ctx_peers(z, count)
+
+    def hop(a, b, base, peer):
+        return send(a, b, zs.at[base, peer], zr.at[base, z], ctx=peer)
+
+    def landed(b, base, peer):
+        return send(b, b, zs.at[base, peer], zr.at[base, peer], ctx=peer)
+
+    load_far = pltpu.make_async_copy(terms.at[:, quarter(far)], tq.at[1], loc.at[0])
+    load_own = pltpu.make_async_copy(terms.at[:, quarter(q)], tq.at[0], loc.at[1])
+    load_far.start()
+    load_own.start()
+    meet([{"ctx": p} for p in to] + [{"tp": q ^ r} for r in (1, 2, 3)] + [{"shard": other}])
+
+    near_far = [remote(terms.at[c, quarter(q ^ 3)], near.at[1, c], tp=mate) for c in range(count)]
+    near_own = [remote(terms.at[c, quarter(mate)], near.at[0, c], tp=mate) for c in range(count)]
+    qkv_in = remote(g_qkv.at[other], qkv_take, shard=other)
+    for p in to:
+        hop(own_out.at[p], result.at[z, mine], 0, p).start()
+    put_out = pltpu.make_async_copy(own_out.at[z], result.at[z, mine], loc.at[2])
+    put_out.start()
+    load_far.wait()
+    from_far = []
+    for c in range(count):
+        arrive(near_far[c])
+        relay[c] = (tq[1, c].astype(F32) + near[1, c].astype(F32)).astype(BF)
+        from_far.append(remote(relay.at[c], away.at[c], tp=far))
+    n_in, n_both = x_give.shape[0], y_give.shape[0]
+    give = pl.ds(pl.multiple_of(other * n_in, n_in), n_in)
+    keep = pl.ds(pl.multiple_of(x * n_in, n_in), n_in)
+    add_rows(x_give, (keep_y.at[give], in_y.at[give]))
+    x_in = remote(x_give, x_take, shard=other)
+    add_rows(y_give, (keep_x.at[1], in_x.at[1]))
+    y_in = remote(y_give, y_take, tp=far)
+
+    def share(ref, base, own):
+        blocks = [remote(own, ref.at[z, mine], tp=far)]
+        remote(own, ref.at[z, mine], tp=mate)
+
+        def step(k):
+            at = ref.at[to[k], mine]
+            landed(at, base, to[k]).wait_recv()
+            blocks.append(remote(at, at, tp=far))
+            remote(at, at, tp=mate)
+
+        def finish(k):
+            arrive(blocks[k])
+            at = ref.at[z if k == 0 else to[k - 1], far_rows]
+            remote(at, at, tp=mate)
+
+        return step, finish
+
+    out_step, out_finish = share(result, 0, own_out.at[z])
+    load_own.wait()
+    column = jnp.zeros((1, width), F32)
+    for c in range(count):
+        arrive(near_own[c])
+        arrive(from_far[c])
+        grad = gjs[c * rows : (c + 1) * rows, :] + tq[0, c].astype(F32) + near[0, c].astype(F32) + away[c].astype(F32)
+        low[c] = grad.astype(BF)
+        column = column + jnp.sum(grad, axis=0, keepdims=True)
+    for p in to:
+        hop(low.at[p], gtok.at[z, mine], 1, p).start()
+    put_tok = pltpu.make_async_copy(low.at[z], gtok.at[z, mine], loc.at[3])
+    put_tok.start()
+    seqs = (totals.shape[0] - 8) // 2
+    small[0] = jnp.zeros(small.shape[1:], F32)
+    small[0, pl.ds(x * seqs + z, 1), :] = column
+    small[0, 2 * seqs : 2 * seqs + 4, :] = sums[0:4, :]
+    small_tp[pl.ds(q, 1)] = small[0][None]
+    tp_small = [remote(small.at[0], small_tp.at[q], tp=q ^ r) for r in (1, 2, 3)]
+    tok_step, tok_finish = share(gtok, 1, low.at[z])
+    for k in range(count - 1):
+        out_step(k)
+
+    arrive(qkv_in)
+    add_rows(m_qkv, (g_qkv.at[x], qkv_take))
+    inner = (z == 1) | (z == 2)
+    outer = (z == 0) | (z == 3)
+    sets = {"qkv": (m_qkv, box_qkv, mid_qkv, f_qkv, o_qkv), "in": (m_in, box_in, mid_in, f_in, o_in),
+            "both": (m_both, box_both, mid_both, f_both, o_both)}
+    plan = []
+    for name in ("qkv", "in", "both"):
+        total = sets[name][0].shape[0]
+        step = chunks[name]
+        for i in range(total // step):
+            plan.append((sets[name], pl.ds(i * step, step)))
+
+    def toward(k):
+        (m, box, _, _, _), r = plan[k]
+        return send(m.at[r], box.at[r], cs.at[0, k], cr.at[0, k], ctx=z ^ 1)
+
+    def across(k):
+        (m, _, mid, _, _), r = plan[k]
+        return send(m.at[r], mid.at[r], cs.at[1, k], cr.at[1, k], ctx=3 - z)
+
+    def back(k):
+        (_, _, _, f, _), r = plan[k]
+        return send(f.at[r], f.at[r], cs.at[2, k], cr.at[2, k], ctx=z ^ 1)
+
+    def begin(k):
+        @pl.when(outer)
+        def _():
+            toward(k).start()
+
+    def join(k):
+        @pl.when(inner)
+        def _():
+            (m, box, _, _, _), r = plan[k]
+            toward(k).wait_recv()
+            add_rows(m.at[r], (m.at[r], box.at[r]))
+            across(k).start()
+
+    def settle(k):
+        @pl.when(inner)
+        def _():
+            (m, _, mid, f, _), r = plan[k]
+            across(k).wait_recv()
+            add_rows(f.at[r], (m.at[r], mid.at[r]))
+            back(k).start()
+
+    first_in = sum(1 for entry in plan if entry[0] is sets["qkv"])
+    first_both = first_in + sum(1 for entry in plan if entry[0] is sets["in"])
+    last = len(plan)
+    for k in range(first_in):
+        begin(k)
+    arrive(x_in)
+    add_rows(m_in, (keep_y.at[keep], in_y.at[keep], x_take))
+    for k in range(first_in, first_both):
+        begin(k)
+    arrive(y_in)
+    add_rows(m_both, (keep_x.at[0], in_x.at[0], y_take))
+    for k in range(first_both, last):
+        begin(k)
+    for copy in tp_small:
+        arrive(copy)
+    small[1] = small_tp[0] + small_tp[1] + small_tp[2] + small_tp[3]
+    small_z[pl.ds(z, 1)] = small[1][None]
+    for p in to:
+        hop(small.at[1], small_z.at[z], 2, p).start()
+    join(0)
+    for k in range(1, last):
+        join(k)
+        settle(k - 1)
+        if k == 2:
+            for j in range(count):
+                out_finish(j)
+        if k in (3, 4, 5):
+            tok_step(k - 3)
+        if k == 5:
+            for p in to:
+                landed(small_z.at[p], 2, p).wait_recv()
+            small[2] = small_z[0] + small_z[1] + small_z[2] + small_z[3]
+            small_x[pl.ds(x, 1)] = small[2][None]
+            x_small = remote(small.at[2], small_x.at[x], shard=other)
+    settle(last - 1)
+    for k in range(count):
+        tok_finish(k)
+    arrive(x_small)
+    totals[...] = small_x[0] + small_x[1]
+    for k in range(last):
+        (_, _, _, f, o), r = plan[k]
+
+        @pl.when(outer)
+        def _():
+            back(k).wait_recv()
+
+        add_rows(o.at[r], (f.at[r],))
+    for k in range(last):
+        @pl.when(outer)
+        def _():
+            toward(k).wait_send()
+
+        @pl.when(inner)
+        def _():
+            across(k).wait_send()
+            back(k).wait_send()
+    for copy in every:
+        copy.wait_send()
+        if all(copy is not e for e in early):
+            copy.wait_recv()
+    for p in to:
+        hop(own_out.at[p], result.at[z, mine], 0, p).wait_send()
+        hop(low.at[p], gtok.at[z, mine], 1, p).wait_send()
+        hop(small.at[1], small_z.at[z], 2, p).wait_send()
+    put_out.wait()
+    put_tok.wait()
+
+
+def tail(terms, gjs, sums, own_out, in_y, keep_y, in_x, keep_x, g_qkv, seqs, ident):
+    count, length, width = terms.shape
+    rows = own_out.shape[1]
+    sem = pltpu.SemaphoreType.DMA
+    shape = jax.ShapeDtypeStruct
+    vmem, hbm = pl.BlockSpec(memory_space=pltpu.VMEM), pl.BlockSpec(memory_space=pl.ANY)
+    n_in, n_both, n_qkv = (in_y.shape[0] // 2, width), in_x.shape[1:], g_qkv.shape[1:]
+    three = (n_in, n_both, n_qkv)
+    small = (2 * seqs + 8, width)
+    low = lambda *s: pltpu.VMEM(s, BF)
+    return pl.pallas_call(
+        functools.partial(tail_kernel, {"qkv": n_qkv[0] // 2, "in": n_in[0] // 2, "both": n_both[0] // 5}),
+        out_shape=(
+            shape((count, length, width), BF), shape((count, length, width), BF),
+            shape(n_in, F32), shape(n_both, F32), shape(n_qkv, F32), shape(small, F32),
+        ),
+        in_specs=[hbm] + [vmem] * 8,
+        out_specs=[hbm, hbm, vmem, vmem, vmem, vmem],
+        scratch_shapes=[
+            low(2, count, rows, width), low(2, count, rows, width), low(count, rows, width), low(count, rows, width),
+            low(count, rows, width), low(*n_in), low(*n_in), low(*n_both), low(*n_both), low(*n_qkv),
+        ] + [low(*n) for n in three] * 4 + [
+            pltpu.VMEM((3,) + small, F32), pltpu.VMEM((4,) + small, F32), pltpu.VMEM((count,) + small, F32), pltpu.VMEM((2,) + small, F32),
+            sem((4,)), sem((3, count)), sem((3, count)), sem((3, 16)), sem((3, 16)), sem((48,)), sem((48,)),
+        ],
+        compiler_params=pltpu.CompilerParams(collective_id=ident, has_side_effects=True),
+        name="tail",
+    )(terms, gjs, sums, own_out, in_y, keep_y, in_x, keep_x, g_qkv)
 
 
 def norm(rows):
@@ -561,36 +1070,48 @@
     def tp_shift(v, bit):
         return lax.ppermute(v, "tp", [(i, i ^ bit) for i in range(tp)])
 
-    token_rows, own_cot, seg = spread(
-        tokens, [cotangent, segments.reshape(seqs, length // 128, 128)], length,
-        [(ctx, rows, width), (ctx, length // 128, 128)], 0,
-    )
+    n_out, n_in, n_down = (shards * w.shape[0] for w in (w_out, w_in, w_down))
+    cuts = (0, w_out.shape[0], w_out.shape[0] + w_in.shape[0], w_out.shape[0] + w_in.shape[0] + w_down.shape[0])
+    n1, n2 = w_time1.shape[0], w_time2.shape[0]
+    blocks = segments.reshape(seqs, length // 128, 128)
+    qkv_flat = w_qkv.reshape(-1, 3 * local)
+    pairs = jnp.concatenate([norm_gains, norm_shifts], axis=1).astype(F32)
+    if shards == 2:
+        feats = time_features(timesteps, n1 * shards).astype(BF).astype(F32)
+        rows8 = jnp.zeros((8, n1 * shards), F32).at[:seqs].set(feats)
+        affine = jnp.zeros((8, n2), F32).at[:4].set(pairs.T[jnp.array([0, 2, 1, 3])])
+        token_rows, own_cot, seg, out_w, in_w, down_w, qkv_w, affine, te, time_pre, own_hidden = front(
+            tokens, cotangent, blocks, w_out, w_in, w_down, qkv_flat, affine, rows8, w_time1, w_time2, 0
+        )
+        feats = shard_gather(feats).reshape(-1, n1 * shards).astype(BF)
+        own_feats = lax.dynamic_slice_in_dim(feats, x * n1, n1, axis=1)
+        out_w = out_w.reshape(tp * n_out, width)
+        in_w = in_w.reshape(tp, n_in, width)
+        down_w = down_w.reshape(tp, n_down, width)
+        qkv_w = qkv_w.reshape(width, 3 * local)
+        affine = jnp.concatenate([affine[0], affine[1]], axis=1)
+    else:
+        token_rows, own_cot, seg = spread(
+            tokens, [cotangent, blocks], length, [(ctx, rows, width), (ctx, length // 128, 128)], 0,
+        )
+        base = jnp.concatenate([shard_gather(w).reshape(-1, width) for w in (w_out, w_in, w_down)], axis=0)
+        away = tp_shift(base, 2)
+        slots = jnp.stack([base, tp_shift(base, 1), away, tp_shift(away, 1)])
+        out_w = slots[:, :n_out].reshape(tp * n_out, width)
+        in_w = slots[:, n_out : n_out + n_in]
+        down_w = slots[:, n_out + n_in :]
+        qkv_w = shard_gather(qkv_flat).reshape(width, 3 * local)
+        affine = shard_gather(pairs).reshape(width, 4).T[jnp.array([0, 2, 1, 3])]
+        feats = time_features(shard_gather(timesteps).reshape(-1), n1 * shards).astype(BF)
+        own_feats = lax.dynamic_slice_in_dim(feats, x * n1, n1, axis=1)
+        time_pre = shard_sum(dot(own_feats, w_time1))
+        time_hidden = silu_fn(time_pre).astype(BF)
+        own_hidden = lax.dynamic_slice_in_dim(time_hidden, x * n2, n2, axis=1)
+        time_embed = shard_sum(dot(own_hidden, w_time2))
+        te = lax.dynamic_slice_in_dim(time_embed, x * seqs + z, 1, axis=0)
     own_tok = lax.dynamic_slice_in_dim(token_rows, q * rows, rows, axis=1).reshape(ctx * rows, width)
     own_cot = own_cot.reshape(ctx * rows, width)
     seg = seg.reshape(full)
-
-    pack = jnp.concatenate([w_out, w_in, w_down], axis=0)
-    pair = shard_gather(pack)
-    cuts = (0, w_out.shape[0], w_out.shape[0] + w_in.shape[0], pack.shape[0])
-    base = jnp.concatenate([pair[:, cuts[i] : cuts[i + 1]].reshape(-1, width) for i in range(3)], axis=0)
-    away = tp_shift(base, 2)
-    slots = jnp.stack([base, tp_shift(base, 1), away, tp_shift(away, 1)])
-    n_out, n_in, n_down = (shards * (cuts[i + 1] - cuts[i]) for i in range(3))
-    out_w = slots[:, :n_out].reshape(tp * n_out, width)
-    in_w = slots[:, n_out : n_out + n_in]
-    down_w = slots[:, n_out + n_in :]
-    qkv_w = shard_gather(w_qkv.reshape(-1, 3 * local)).reshape(width, 3 * local)
-    affine = shard_gather(jnp.concatenate([norm_gains, norm_shifts], axis=1)).reshape(width, 4)
-    affine = affine.astype(F32).T[jnp.array([0, 2, 1, 3])]
-
-    feats = time_features(shard_gather(timesteps).reshape(-1), w_time1.shape[0] * shards).astype(BF)
-    n1, n2 = w_time1.shape[0], w_time2.shape[0]
-    own_feats = lax.dynamic_slice_in_dim(feats, x * n1, n1, axis=1)
-    time_pre = shard_sum(dot(own_feats, w_time1))
-    time_hidden = silu_fn(time_pre).astype(BF)
-    own_hidden = lax.dynamic_slice_in_dim(time_hidden, x * n2, n2, axis=1)
-    time_embed = shard_sum(dot(own_hidden, w_time2))
-    te = lax.dynamic_slice_in_dim(time_embed, x * seqs + z, 1, axis=0)
 
     mixed_low = (token_rows.reshape(full, width).astype(F32) + te).astype(BF)
     joint_t = contract(qkv_w, mixed_low, 0, 1).astype(BF)
@@ -602,19 +1123,33 @@
     out_own, gjs, gatt, g_out, g_in, g_down, sums = middle(
         att_own, own_tok, te, affine, own_cot, out_w, in_w, down_w
     )
-    (result,) = spread(out_own.reshape(ctx, rows, width), [], length, [], 2)
-    got = swap(gatt.reshape(tp, local, ctx * rows), False, True, 3)
+    out_own = out_own.reshape(ctx, rows, width)
+    gatt = gatt.reshape(tp, local, ctx * rows)
+    g_out = g_out.reshape(tp, n_out, width)
+    fast = shards == 2 and ctx == 4
+    if fast:
+        got, send_y, keep_y, send_x, keep_x = turn(gatt, g_out, g_in, g_down, 3)
+        in_y = tp_shift(send_y, 2)
+        in_x = lax.ppermute(send_x, "shard", [(0, 1), (1, 0)])
+    else:
+        (result,) = spread(out_own, [], length, [], 2)
+        got = swap(gatt, False, True, 3)
     lo, hi = key_ranges(seg, length, 256)
     dq, dkv = attend_back(joint_t, aq, ak, att, got, lse, lo, hi, heads, HEAD_DIM, tp, length, 256)
     grad_t = jnp.concatenate([dq, dkv], axis=0)
     g_qkv = contract(mixed_low, grad_t, 0, 1).astype(BF)
     terms = contract(grad_t, qkv_w, 0, 1).astype(BF).reshape(ctx, length, width)
-    grad_own = gjs.reshape(ctx, rows, width) + fold(terms, 4)
-    (grad_tokens,) = spread(grad_own.astype(BF), [], length, [], 5)
-
-    total = jnp.zeros((seqs * shards, width), F32)
-    total = lax.dynamic_update_slice_in_dim(total, jnp.sum(grad_own, axis=(0, 1))[None], x * seqs + z, 0)
-    total = lax.psum(jnp.concatenate([total, sums[:4]], axis=0), ("shard", "ctx", "tp"))
+    if fast:
+        result, grad_tokens, piece_in, piece_both, qkv_piece, total = tail(
+            terms, gjs, sums, out_own, in_y, keep_y, in_x, keep_x, g_qkv.reshape(shards, width // shards, 3 * local), seqs, 4
+        )
+        total = total[: seqs * shards + 4]
+    else:
+        grad_own = gjs.reshape(ctx, rows, width) + fold(terms, 4)
+        (grad_tokens,) = spread(grad_own.astype(BF), [], length, [], 5)
+        total = jnp.zeros((seqs * shards, width), F32)
+        total = lax.dynamic_update_slice_in_dim(total, jnp.sum(grad_own, axis=(0, 1))[None], x * seqs + z, 0)
+        total = lax.psum(jnp.concatenate([total, sums[:4]], axis=0), ("shard", "ctx", "tp"))
     grad_embed = total[: seqs * shards].astype(BF)
     own_pre = lax.dynamic_slice_in_dim(time_pre, x * n2, n2, axis=1)
     grad_pre = jax.vjp(silu_fn, own_pre)[1](contract(grad_embed, w_time2, 1, 1))[0].astype(BF)
@@ -626,20 +1161,24 @@
     g_gains = jnp.stack([affine_sums[0], affine_sums[2]], axis=1)
     g_shifts = jnp.stack([affine_sums[1], affine_sums[3]], axis=1)
 
-    grads = jnp.concatenate([g_out.reshape(tp, n_out, width), g_in, g_down], axis=1)
-    near = tp_shift(jnp.stack([grads[1], grads[3]]), 1)
-    half0 = (grads[0].astype(F32) + near[0].astype(F32))
-    half2 = (grads[2].astype(F32) + near[1].astype(F32)).astype(BF)
-    whole = (half0 + tp_shift(half2, 2).astype(F32)).astype(BF)
-    marks = (0, n_out, n_out + n_in, n_out + n_in + n_down)
-    whole = jnp.concatenate([whole[marks[i] : marks[i + 1]].reshape(shards, -1, width) for i in range(3)], axis=1)
-    piece = shard_scatter(whole).astype(BF)
-    qkv_piece = shard_scatter(g_qkv.reshape(shards, width // shards, 3 * local)).astype(BF)
-    piece = lax.psum(piece, "ctx").astype(F32)
-    qkv_piece = lax.psum(qkv_piece, "ctx").astype(F32)
+    if fast:
+        piece_out, piece_down = piece_both[: cuts[1]], piece_both[cuts[1] :]
+    else:
+        grads = jnp.concatenate([g_out, g_in, g_down], axis=1)
+        near = tp_shift(jnp.stack([grads[1], grads[3]]), 1)
+        half0 = (grads[0].astype(F32) + near[0].astype(F32))
+        half2 = (grads[2].astype(F32) + near[1].astype(F32)).astype(BF)
+        whole = (half0 + tp_shift(half2, 2).astype(F32)).astype(BF)
+        marks = (0, n_out, n_out + n_in, n_out + n_in + n_down)
+        whole = jnp.concatenate([whole[marks[i] : marks[i + 1]].reshape(shards, -1, width) for i in range(3)], axis=1)
+        piece = shard_scatter(whole).astype(BF)
+        qkv_piece = shard_scatter(g_qkv.reshape(shards, width // shards, 3 * local)).astype(BF)
+        piece = lax.psum(piece, "ctx").astype(F32)
+        qkv_piece = lax.psum(qkv_piece, "ctx").astype(F32)
+        piece_out, piece_in, piece_down = piece[: cuts[1]], piece[cuts[1] : cuts[2]], piece[cuts[2] :]
     return (
         result, grad_tokens.astype(F32), g_time1, g_time2, qkv_piece.reshape(w_qkv.shape),
-        piece[: cuts[1]], piece[cuts[1] : cuts[2]], piece[cuts[2] :], g_gains, g_shifts,
+        piece_out, piece_in, piece_down, g_gains, g_shifts,
     )
 
 

time: 569 us -> 350 us (0.62)
  waiting for transfers between devices: 67.9 us -> 0.01 us
  blocking collectives: 39.9 us -> 0 us
  other arithmetic: 54.2 us -> 16.9 us
  Pallas kernels: 313 us -> 282 us
  starting transfers between devices: 32.5 us -> 12.9 us
  between operations: 14.5 us -> 0.87 us
  local copies, waits for them, and re-layouts: 29.4 us -> 23.2 us
    pallas_call x2 -> x1, Pallas kernels: 77.2 us -> 13.5 us  [swap(): pl.pallas_call(functools.partial(swap_kernel, src_abs, dst_abs), out_shap...]
    psum x1 -> x0, blocking collectives: 39.9 us -> none  [body(): lax.psum(jnp.concatenate([total, sums[:4]], axis=0), ('shard', 'ctx', 'tp'))]
    pallas_call x4 -> x3, Pallas kernels: 160 us -> 190 us  [the longest x1 109 us: tail(): pl.pallas_call(functools.partial(tail_kernel, {'qkv': n_qkv[0] // 2, 'in'...]
    ppermute x4 -> x1, waiting for transfers between devices: 30 us -> 0.01 us  [body(): in_x = lax.ppermute(send_x, 'shard', [(0, 1), (1, 0)])]
    ppermute x5 -> x2, waiting for transfers between devices: 29.1 us -> 0.01 us  [shard_gather(): other = lax.ppermute(v, 'shard', [(0, 1), (1, 0)])]
    ppermute x4 -> x1, starting transfers between devices: 19.8 us -> 5.51 us  [body(): in_x = lax.ppermute(send_x, 'shard', [(0, 1), (1, 0)])]
    convert_element_type x4 -> x2, other arithmetic: 12 us -> 0.09 us  [the longest x1 0.08 us: body(): feats = time_features(timesteps, n1 * shards).astype(BF).astype(F32)]
    another operation x5 -> x0, other arithmetic: 10.5 us -> none  [the longest x2 9.88 us: body(): slots = jnp.stack([base, tp_shift(base, 1), away, tp_shift(away, 1)])]
  transfers between devices with their start and end apart: 15 -> 4, of which waited for: 5 -> 0; matrix products, arithmetic and copies ran while one was open for 10% -> 13% of each run, Pallas kernels for 50% -> 49%
where the time goes in v2:
time: 350 us; the launch traced here: 349 us
  Pallas kernels  282 us (81%)
  local copies, waits for them, and re-layouts  23.2 us (7%)
  other arithmetic  16.9 us (5%)
  matrix products  13.9 us (4%)
  starting transfers between devices  12.9 us (4%)
    pallas_call x1, Pallas kernels, tail(): pl.pallas_call(functools.partial(tail_kernel, {'qkv': n_qkv[0] // 2, 'in'...  109 us
    pallas_call x1, Pallas kernels, front(): pl.pallas_call(front_kernel, out_shape=outs, in_specs=[hbm, hbm, vmem, hb...  67.3 us
    pallas_call x1, Pallas kernels, middle(): pl.pallas_call(functools.partial(middle_kernel, chunk), out_shape=(shape(...  29.7 us
    pallas_call x1, Pallas kernels, attend_back(): pl.pallas_call(functools.partial(attend_back_kernel, heads, bk, hd ** (-0...  29.1 us
    pallas_call x1, Pallas kernels, attend(): pl.pallas_call(functools.partial(attend_kernel, heads, bk), out_shape=(ja...  19.1 us
    pallas_call x1, Pallas kernels, turn(): pl.pallas_call(turn_kernel, out_shape=(shape(gatt.shape, BF), shape(g_in....  14 us
    dot_general x6, matrix products, contract(): lax.dot_general(left, right, (((ldim,), (rdim,)), ((), ())), preferred_el...  13.9 us
    pallas_call x1, Pallas kernels, swap(): pl.pallas_call(functools.partial(swap_kernel, src_abs, dst_abs), out_shap...  13.5 us
  transfers between devices with their start and end apart: 4, of which 0 were waited for; matrix products, arithmetic and copies ran while one was open for 13% of the time, Pallas kernels for 49%

profile of v2, /device:TPU:0, one launch (start us, length us, event | category | flops | bytes accessed | tf_op | source)
XLA Modules:
  0.0 349.4 jit_solution(15936564398167815874)
XLA Ops:
  0.7 0.7 convert_element_type.77
  1.3 0.1 fusion.11
  1.4 0.1 fusion.12
  1.5 3.0 collective-permute-start.2
  4.5 0.7 pad_clamp_fusion
  5.1 0.6 scatter.9.feats
  5.7 0.7 convert_bitcast_fusion
  6.4 0.6 gather_fusion
  7.0 0.6 scatter.6.affine
  7.6 1.3 reshape.242.seg
  8.9 2.0 copy.26.w_qkv
  10.9 67.3 %front.1 = (bf16[4,512,768]{2,1,0:T(8,128)(2,1)}, bf16[4,128,768]{2,1,0:T(8,128)(2,1)}, s32[4,4,128]{2,1,0:T(4,128)}, bf16[4,2,96,768]{3,2,1,0:T(8,128)(2,1)}, b...) custom-call(bf16[4,512,768]{2,1,0:T(8,128)(2,1)} %src.1, ...), custom_call_target="tpu_custom_call" | custom-call | tf_op jit(solution)/shard_map/front/pallas_call | solution.py:508
  78.3 0.8 slice.81
  79.0 0.8 slice.80
  79.8 0.7 select_convert_fusion
  80.5 0.7 fusion.1
  81.2 0.7 reduce.4
  81.9 2.5 add_convert_fusion
  84.5 2.4 convolution_convert_fusion.1
  86.9 0.9 slice_multiply_fusion.qt_ref
  87.9 1.3 slice.97.kv_ref
  89.2 0.1 pad.25.clone
  89.3 0.1 pad.24.clone
  89.4 0.7 concatenate.39.aq_ref
  90.1 0.9 constant_dynamic-slice_fusion
  91.0 0.2 convert_reduce_fusion
  91.2 0.6 and_select_fusion
  91.8 0.8 maximum_maximum_fusion.ak_ref
  92.6 19.1 %attend.1 = (bf16[4,192,512]{2,1,0:T(8,128)(2,1)}, f32[3,1,2048]{2,1,0:T(1,128)}) custom-call(s32[4]{0:T(128)} %get-tuple-element.129.lo_ref, s32[4]{0:T(128)} %get-tuple-element.124.hi_ref, bf16[192,2048]{1,0:T(8,128)(2,1)} %slice_multiply_fusion.qt_ref, bf16[384,2048]{1,0:T(8,128)(2,1)} %slice.97.kv_ref, bf16[64,2048]{1,0:T(8,128)(2,1)} %concatenate.39.aq_ref, ...), custom_call_target="tpu_custom_call" | custom-call | flops 3221225472 | bytes 3145728 | tf_op jit(solution)/shard_map/attend/pallas_call | solution.py:100
  111.8 13.5 %swap.1 = bf16[4,192,512]{2,1,0:T(8,128)(2,1)} custom-call(bf16[4,192,512]{2,1,0:T(8,128)(2,1)} %get-tuple-element.71.src.ot_ref), custom_call_target="tpu_custom_call" | custom-call | tf_op jit(solution)/shard_map/swap/pallas_call | solution.py:544
  125.3 0.6 pad_maximum_fusion.affine
  125.9 29.7 %middle.1 = (bf16[512,768]{1,0:T(8,128)(2,1)}, f32[512,768]{1,0:T(8,128)}, bf16[768,512]{1,0:T(8,128)(2,1)}, bf16[768,768]{1,0:T(8,128)(2,1)}, bf16[4,768,768]{2...) custom-call(bf16[768,512]{1,0:T(8,128)(2,1)} %bitcast.62, bf16[512,768]{1,0:T(8,128)(2,1)} %bitcast.61, ...), custom_call_target="tpu_custom_call" | custom-call | flops 16307453952 | bytes 56623104 | tf_op jit(solution)/shard_map/middle/pallas_call | solution.py:1020
  155.6 14.0 %turn.1 = (bf16[4,192,512]{2,1,0:T(8,128)(2,1)}, bf16[768,768]{1,0:T(8,128)(2,1)}, bf16[768,768]{1,0:T(8,128)(2,1)}, bf16[2,480,768]{2,1,0:T(8,128)(2,1)}, bf16[2,480,768]{2,1,0:T(8,128)(2,1)}) custom-call(bf16[4,192,512]{2,1,0:T(8,128)(2,1)} %bitcast.60, bf16[4,192,768]{2,1,0:T(8,128)(2,1)} %bitcast.57, bf16[4,768,768]{2,1,0:T(8,128)(2,1)} %get-tuple-element.79.g_in, ...), custom_call_target="tpu_custom_call" | custom-call | tf_op jit(solution)/shard_map/turn/pallas_call | solution.py:681
  169.7 1.3 collective-permute-start
  170.9 5.5 %collective-permute-start.1 = (bf16[2,480,768]{2,1,0:T(8,128)(2,1)}, bf16[2,480,768]{2,1,0:T(8,128)(2,1)}, u32[]{:S(2)}, u32[]{:S(2)}) collective-permute-start(bf16[2,480,768]{2,1,0:T(8,128)(2,1)} %get-tuple-element.90), channel_id=1, source_target_pairs={{0,16},{16,0},{1,17},{17,1},{2,18},{18,2},{3,19},{19,3},{4,20},{20... | collective-permute-start | bytes 4423688 | tf_op jit(solution)/shard_map/ppermute | solution.py:1133
  176.5 2.4 fusion
  178.8 29.1 %attend_back.1 = (bf16[192,2048]{1,0:T(8,128)(2,1)}, bf16[384,2048]{1,0:T(8,128)(2,1)}) custom-call(s32[4]{0:T(128)} %get-tuple-element.128.lo_ref, s32[4]{0:T(128)} %get-tuple-element.125.hi_ref, bf16[192,2048]{1,0:T(8,128)(2,1)} %slice_multiply_fusion.qt_ref, bf16[384,2048]{1,0:T(8,128)(2,1)} %slice.97.kv_ref, bf16[64,2048]{1,0:T(8,128)(2,1)} %concatenate.39.aq_ref, ...), custom_call_target="tpu_custom_call" | custom-call | flops 8053063680 | bytes 6291456 | tf_op jit(solution)/shard_map/attend_back/pallas_call | solution.py:210
  207.9 1.2 constant_dynamic-update-slice_fusion.1
  209.1 0.1 maximum_convert_fusion.1
  209.2 1.6 constant_dynamic-update-slice_fusion
  210.8 0.0 copy-start.3
  210.8 5.5 %convolution_convert_fusion = bf16[2048,768]{1,0:T(8,128)(2,1)} fusion(bf16[576,2048]{1,0:T(8,128)(2,1)S(1)} %constant_dynamic-update-slice_fusion, bf16[768,576]{1,0:T(8,128)(2,1)} %bitcast.77), kind=kOutput, calls=%fused_computation.4 | convolution fusion | flops 1813512192 | bytes 6389760 | tf_op jit(solution)/shard_map/dot_general | solution.py:37
  216.3 2.0 convolution_convert_fusion.2
  218.3 1.3 copy.27
  219.6 0.0 collective-permute-done.2
  219.6 0.0 collective-permute-done.in_y
  219.6 0.0 copy-start.4
  219.7 108.7 %tail.1 = (bf16[4,512,768]{2,1,0:T(8,128)(2,1)}, bf16[4,512,768]{2,1,0:T(8,128)(2,1)}, f32[384,768]{1,0:T(8,128)}, f32[480,768]{1,0:T(8,128)}, f32[384,576]{1,0:T(8,128)}, /*index=5*/f32[16,768]{1,0:T(8,128)}) custom-call(bf16[4,512,768]{2,1,0:T(8,128)(2,1)} %bitcast.55, f32[512,768]{1,0:T(8,128)} %get-tuple-element.85.gjs, ...), custom_call_target="tpu_custom_call" | custom-call | tf_op jit(solution)/shard_map/tail/pallas_call | solution.py:921
  328.4 0.9 slice.89
  329.2 1.0 add_convert_fusion.1
  330.3 3.2 collective-permute-start.3
  333.4 2.1 fusion.3
  335.5 0.1 dynamic-slice_bitcast_fusion.1
  335.6 0.6 pad_maximum_fusion.2
  336.2 0.6 pad_maximum_fusion.1
  336.8 1.7 slice.87
  338.5 1.1 slice.88
  339.6 2.4 copy.28
  342.0 3.2 convert_element_type.92
  345.3 0.0 collective-permute-done.3
  345.3 1.0 fusion.7
  346.3 1.7 copy.32
  347.9 0.4 copy-done.6
  348.4 1.0 copy.33
  (28 shorter events, 0.1 us)
Async XLA Ops:
  1.5 218.1 %collective-permute-start.2 = (bf16[4,128]{1,0:T(4,128)(2,1)S(1)}, bf16[4,128]{1,0:T(4,128)(2,1)S(1)}, u32[]{:S(2)}, u32[]{:S(2)}) collective-permute-start(bf16[4,128]{1,0:T(4,128)(2,1)S(1)} %get-tuple-element.112), channel_id=1, source_target_pairs={{0,16},{16,0},{1,17},{17,1},{2,18},{18,2},{3,19},{19,3},{4,20},{20... | collective-permute-start | bytes 3080 | tf_op jit(solution)/shard_map/ppermute | solution.py:1054
  81.9 2.6 copy-start.11
  86.9 2.5 copy-start.8
  86.9 3.2 copy-start
  86.9 4.1 %copy-start.7 = (s32[4,4,128]{2,1,0:T(4,128)S(1)}, s32[4,4,128]{2,1,0:T(4,128)}, u32[]{:S(2)}) copy-start(s32[4,4,128]{2,1,0:T(4,128)} %get-tuple-element.67) | copy-start | bytes 24580
  169.7 50.0 %collective-permute-start = (bf16[768,768]{1,0:T(8,128)(2,1)}, bf16[768,768]{1,0:T(8,128)(2,1)}, u32[]{:S(2)}, u32[]{:S(2)}) collective-permute-start(bf16[768,768]{1,0:T(8,128)(2,1)} %get-tuple-element.88), channel_id=1, source_target_pairs={{0,2},{1,3},{2,0},{3,1},{4,6},{5,7},{6,4},{7,5},{8,10},{9,11},{10,... | collective-permute-start | bytes 3538952 | tf_op jit(solution)/shard_map/ppermute | solution.py:1071
  170.9 48.7 %collective-permute-start.1 = (bf16[2,480,768]{2,1,0:T(8,128)(2,1)}, bf16[2,480,768]{2,1,0:T(8,128)(2,1)}, u32[]{:S(2)}, u32[]{:S(2)}) collective-permute-start(bf16[2,480,768]{2,1,0:T(8,128)(2,1)} %get-tuple-element.90), channel_id=1, source_target_pairs={{0,16},{16,0},{1,17},{17,1},{2,18},{18,2},{3,19},{19,3},{4,20},{20... | collective-permute-start | bytes 4423688 | tf_op jit(solution)/shard_map/ppermute | solution.py:1133
  210.8 5.5 %copy-start.3 = (bf16[2048,768]{1,0:T(8,128)(2,1)S(1)}, bf16[2048,768]{1,0:T(8,128)(2,1)}, u32[]{:S(2)}) copy-start(bf16[2048,768]{1,0:T(8,128)(2,1)} %fusion) | copy-start | bytes 9437188
  219.6 109.6 %copy-start.4 = (bf16[384,768]{1,0:T(8,128)(2,1)S(1)}, bf16[384,768]{1,0:T(8,128)(2,1)}, u32[]{:S(2)}) copy-start(bf16[384,768]{1,0:T(8,128)(2,1)} %w_time2.1) | copy-start | bytes 1769476
  219.7 109.6 %copy-start.10 = (f32[8,768]{1,0:T(8,128)S(1)}, f32[8,768]{1,0:T(8,128)}, u32[]{:S(2)}) copy-start(f32[8,768]{1,0:T(8,128)} %get-tuple-element.95) | copy-start | bytes 73732
  219.7 113.8 %copy-start.9 = (bf16[8,384]{1,0:T(8,128)(2,1)S(1)}, bf16[8,384]{1,0:T(8,128)(2,1)}, u32[]{:S(2)}) copy-start(bf16[8,384]{1,0:T(8,128)(2,1)} %get-tuple-element.96) | copy-start | bytes 18436
  328.4 10.1 %copy-start.5 = (f32[480,768]{1,0:T(8,128)S(1)}, f32[480,768]{1,0:T(8,128)}, u32[]{:S(2)}) copy-start(f32[480,768]{1,0:T(8,128)} %get-tuple-element.98) | copy-start | bytes 4423684
  330.2 11.8 %copy-start.2 = (bf16[4,512,768]{2,1,0:T(8,128)(2,1)S(1)}, bf16[4,512,768]{2,1,0:T(8,128)(2,1)}, u32[]{:S(2)}) copy-start(bf16[4,512,768]{2,1,0:T(8,128)(2,1)} %get-tuple-element.93) | copy-start | bytes 9437188
  330.3 15.0 %collective-permute-start.3 = (bf16[8,384]{1,0:T(8,128)(2,1)S(1)}, bf16[8,384]{1,0:T(8,128)(2,1)S(1)}, u32[]{:S(2)}, u32[]{:S(2)}) collective-permute-start(bf16[8,384]{1,0:T(8,128)(2,1)S(1)} %add_convert_fusion.1), channel_id=1, source_target_pairs={{0,16},{16,0},{1,17},{17,1},{2,18},{18,2},{3,19},{19,3},{4,20},{20... | collective-permute-start | bytes 18440 | tf_op jit(solution)/shard_map/ppermute | solution.py:1054
  342.0 4.2 %copy-start.1 = (bf16[4,512,768]{2,1,0:T(8,128)(2,1)S(1)}, bf16[4,512,768]{2,1,0:T(8,128)(2,1)}, u32[]{:S(2)}) copy-start(bf16[4,512,768]{2,1,0:T(8,128)(2,1)} %get-tuple-element.140) | copy-start | bytes 9437188
  346.3 2.1 copy-start.6
